TPU v7x, 32 devices: a whole 2x2x4 slice. The times are simulated.
32 devices in a mesh: dp: 8 (over z, x), mp: 4 (over y, core).
Axes of the slice: x: 2, y: 2, z: 4, core: 2. Of those that a mesh axis runs over, the one named last changes fastest.
Arguments:
- text_blocks: bfloat16 [256, 64, 768], P(('dp', 'mp')), may hold values from -6 to 6
- visual_blocks: bfloat16 [256, 40, 768], P(('dp', 'mp')), may hold values from -6 to 6
- drop_flags: int32 [256, 2], P('dp'), may hold values 0 or 1
- qkv_weight: bfloat16 [4, 768, 3, 768], P(None, None, None, 'mp'), may hold values from -0.21875 to 0.21875
- out_weight: bfloat16 [4, 768, 768], P(None, 'mp'), may hold values from -0.625 to 0.625
- up_weight: bfloat16 [2, 768, 3072], P(None, None, 'mp'), may hold values from -0.21875 to 0.21875
- down_weight: bfloat16 [2, 3072, 768], P(None, 'mp'), may hold values from -0.109375 to 0.109375
- norm_gain: float32 [6, 768], replicated, may hold values from 0.5 to 1.5
- norm_shift: float32 [6, 768], replicated, may hold values from -3 to 3
- text_cotangent: bfloat16 [256, 64, 768], P(('dp', 'mp')), may hold values from -6 to 6
- visual_cotangent: bfloat16 [256, 40, 768], P(('dp', 'mp')), may hold values from -6 to 6
Outputs:
- text_output: bfloat16 [256, 64, 768], P(('dp', 'mp'))
- visual_output: bfloat16 [256, 40, 768], P(('dp', 'mp'))
- text_gradient: bfloat16 [256, 64, 768], P(('dp', 'mp'))
- visual_gradient: bfloat16 [256, 40, 768], P(('dp', 'mp'))
- qkv_gradient: float32 [4, 768, 3, 768], P(None, None, None, 'mp')
- out_gradient: float32 [4, 768, 768], P(None, 'mp')
- up_gradient: float32 [2, 768, 3072], P(None, None, 'mp')
- down_gradient: float32 [2, 3072, 768], P(None, 'mp')
- gain_gradient: float32 [6, 768], replicated
- shift_gradient: float32 [6, 768], replicated
Inputs may be any that keep to these rules, and one draw needn't show every extreme that they name: drop_flags[:, 0] = 1 marks a page whose text is absent, drop_flags[:, 1] = 1 one whose visual blocks are absent.
All inputs are finite; a program needn't handle non-finite values.
Results may differ from a plain program's by a relative error of at most 0.025.
Values may be sent and summed in bfloat16 or wider, within the bound.
No kernel may reach another device: no remote copies, remote signals or barrier semaphores. Data moves between devices by JAX's collectives and lax.ppermute only.
A program may use at most 256 MiB of HBM per device.

v0:
```python
import jax
import jax.numpy as jnp
from jax import lax
from jax.sharding import PartitionSpec as P

HEAD = 64


EPSILON = 1e-05


def normalize(values, gain, shift):
    center = values - jnp.mean(values, axis=-1, keepdims=True)
    spread = jnp.mean(center * center, axis=-1, keepdims=True)
    return center * lax.rsqrt(spread + EPSILON) * gain + shift


def linear(activation, weight):
    return jnp.einsum("pld,de->ple", activation, weight, preferred_element_type=jnp.float32)


def linear_back(gradient, weight):
    return jnp.einsum("ple,de->pld", gradient, weight, preferred_element_type=jnp.float32)


def weight_grad(activation, gradient):
    return jnp.einsum("pld,ple->de", activation, gradient, preferred_element_type=jnp.float32)


def split_heads(values):
    return values.reshape(values.shape[0], values.shape[1], values.shape[2] // HEAD, HEAD)


def merge_heads(values):
    return values.reshape(values.shape[0], values.shape[1], values.shape[2] * values.shape[3])


def score_block(queries, key_block):
    raw = jnp.einsum(
        "pqhe,pkhe->phqk",
        split_heads(queries),
        split_heads(key_block),
        preferred_element_type=jnp.float32,
    )
    return raw * HEAD ** (-0.5)


def attend_context(query_side, key_side, weight_block, keep_mask):
    queries = linear(query_side, weight_block[:, 0]).astype(jnp.bfloat16)
    key_block = linear(key_side, weight_block[:, 1]).astype(jnp.bfloat16)
    value_block = linear(key_side, weight_block[:, 2]).astype(jnp.bfloat16)
    scores = score_block(queries, key_block)
    row_max = jnp.max(scores, axis=-1, keepdims=True)
    log_total = row_max + jnp.log(jnp.sum(jnp.exp(scores - row_max), axis=-1, keepdims=True))
    probability = jnp.exp(scores - log_total).astype(jnp.bfloat16)
    context = merge_heads(
        jnp.einsum(
            "phqk,pkhe->pqhe",
            probability,
            split_heads(value_block),
            preferred_element_type=jnp.float32,
        )
    )
    if keep_mask is not None:
        context = context * keep_mask[:, None, None]
    context = context.astype(jnp.bfloat16)
    return (context, (queries, key_block, value_block, log_total, context))


def attend_back(query_side, key_side, weight_block, out_block, keep_mask, saved, out_grad):
    queries, key_block, value_block, log_total, context = saved
    out_weight_grad = weight_grad(context, out_grad)
    context_grad = linear_back(out_grad, out_block).astype(jnp.bfloat16)
    if keep_mask is not None:
        context_grad = context_grad * keep_mask[:, None, None].astype(jnp.bfloat16)
    probability = jnp.exp(score_block(queries, key_block) - log_total)
    heads_grad = split_heads(context_grad)
    prob_grad = jnp.einsum(
        "pqhe,pkhe->phqk", heads_grad, split_heads(value_block), preferred_element_type=jnp.float32
    )
    value_grad = merge_heads(
        jnp.einsum(
            "phqk,pqhe->pkhe",
            probability.astype(jnp.bfloat16),
            heads_grad,
            preferred_element_type=jnp.float32,
        )
    ).astype(jnp.bfloat16)
    score_grad = (
        probability * (prob_grad - jnp.sum(prob_grad * probability, axis=-1, keepdims=True))
    ).astype(jnp.bfloat16)
    query_grad = (
        merge_heads(
            jnp.einsum(
                "phqk,pkhe->pqhe",
                score_grad,
                split_heads(key_block),
                preferred_element_type=jnp.float32,
            )
        )
        * HEAD ** (-0.5)
    ).astype(jnp.bfloat16)
    key_grad = (
        merge_heads(
            jnp.einsum(
                "phqk,pqhe->pkhe",
                score_grad,
                split_heads(queries),
                preferred_element_type=jnp.float32,
            )
        )
        * HEAD ** (-0.5)
    ).astype(jnp.bfloat16)
    in_weight_grad = jnp.stack(
        [
            weight_grad(query_side, query_grad),
            weight_grad(key_side, key_grad),
            weight_grad(key_side, value_grad),
        ],
        axis=1,
    )
    query_back = linear_back(query_grad, weight_block[:, 0])
    key_back = linear_back(key_grad, weight_block[:, 1]) + linear_back(
        value_grad, weight_block[:, 2]
    )
    return (in_weight_grad, out_weight_grad, query_back, key_back)


def feed_forward(activation, up_block, down_block):
    before = linear(activation, up_block)
    hidden = jax.nn.gelu(before).astype(jnp.bfloat16)
    return (linear(hidden, down_block), (before, hidden))


def feed_back(activation, up_block, down_block, saved, out_grad):
    before, hidden = saved
    down_grad = weight_grad(hidden, out_grad)
    hidden_grad = linear_back(out_grad, down_block)
    gelu_pull = jax.vjp(jax.nn.gelu, before)[1]
    before_grad = gelu_pull(hidden_grad)[0].astype(jnp.bfloat16)
    up_grad = weight_grad(activation, before_grad)
    return (up_grad, down_grad, linear_back(before_grad, up_block))


def per_device(
    text_blocks,
    visual_blocks,
    drop_flags,
    qkv_weight,
    out_weight,
    up_weight,
    down_weight,
    norm_gain,
    norm_shift,
    text_cotangent,
    visual_cotangent,
):
    keep_text = (1 - drop_flags[:, 0]).astype(jnp.float32)
    keep_visual = (1 - drop_flags[:, 1]).astype(jnp.float32)
    text_now = text_blocks.astype(jnp.float32)
    visual_now = visual_blocks.astype(jnp.float32)
    inputs = []
    gathered = []
    saved = []
    for sublayer in range(3):
        inputs.append((text_now, visual_now))
        text_norm = normalize(text_now, norm_gain[2 * sublayer], norm_shift[2 * sublayer]).astype(
            jnp.bfloat16
        )
        visual_norm = normalize(
            visual_now, norm_gain[2 * sublayer + 1], norm_shift[2 * sublayer + 1]
        ).astype(jnp.bfloat16)
        text_rows, visual_rows = (
            lax.all_gather(text_norm, "mp", axis=0, tiled=True),
            lax.all_gather(visual_norm, "mp", axis=0, tiled=True),
        )
        gathered.append((text_rows, visual_rows))
        text_part = None
        visual_part = None
        if sublayer < 2:
            if sublayer == 0:
                text_context, text_saved = attend_context(
                    text_rows, visual_rows, qkv_weight[0], keep_visual
                )
                visual_context, visual_saved = attend_context(
                    visual_rows, text_rows, qkv_weight[1], keep_text
                )
            else:
                text_context, text_saved = attend_context(text_rows, text_rows, qkv_weight[2], None)
                visual_context, visual_saved = attend_context(
                    visual_rows, visual_rows, qkv_weight[3], None
                )
            text_part = linear(text_context, out_weight[2 * sublayer])
            visual_part = linear(visual_context, out_weight[2 * sublayer + 1])
        else:
            text_part, text_saved = feed_forward(text_rows, up_weight[0], down_weight[0])
            visual_part, visual_saved = feed_forward(visual_rows, up_weight[1], down_weight[1])
        text_added, visual_added = (
            lax.psum_scatter(
                text_part.astype(jnp.bfloat16), "mp", scatter_dimension=0, tiled=True
            ).astype(jnp.float32),
            lax.psum_scatter(
                visual_part.astype(jnp.bfloat16), "mp", scatter_dimension=0, tiled=True
            ).astype(jnp.float32),
        )
        saved.append((text_saved, visual_saved))
        text_now = text_now + text_added
        visual_now = visual_now + visual_added
    text_output = text_now.astype(jnp.bfloat16)
    visual_output = visual_now.astype(jnp.bfloat16)
    text_back = text_cotangent.astype(jnp.float32)
    visual_back = visual_cotangent.astype(jnp.float32)
    in_parts = [None, None, None, None]
    out_parts = [None, None, None, None]
    gain_parts = [None, None, None, None, None, None]
    shift_parts = [None, None, None, None, None, None]
    up_grads = None
    down_grads = None
    for sublayer in (2, 1, 0):
        text_branch, visual_branch = (
            lax.all_gather(text_back.astype(jnp.bfloat16), "mp", axis=0, tiled=True),
            lax.all_gather(visual_back.astype(jnp.bfloat16), "mp", axis=0, tiled=True),
        )
        text_rows, visual_rows = gathered[sublayer]
        text_saved, visual_saved = saved[sublayer]
        if sublayer == 2:
            up_text, down_text, text_part = feed_back(
                text_rows, up_weight[0], down_weight[0], text_saved, text_branch
            )
            up_visual, down_visual, visual_part = feed_back(
                visual_rows, up_weight[1], down_weight[1], visual_saved, visual_branch
            )
            up_grads = jnp.stack([up_text, up_visual])
            down_grads = jnp.stack([down_text, down_visual])
        elif sublayer == 1:
            in_parts[2], out_parts[2], query_back, key_back = attend_back(
                text_rows, text_rows, qkv_weight[2], out_weight[2], None, text_saved, text_branch
            )
            text_part = query_back + key_back
            in_parts[3], out_parts[3], query_back, key_back = attend_back(
                visual_rows,
                visual_rows,
                qkv_weight[3],
                out_weight[3],
                None,
                visual_saved,
                visual_branch,
            )
            visual_part = query_back + key_back
        else:
            in_parts[0], out_parts[0], text_query_back, visual_key_back = attend_back(
                text_rows,
                visual_rows,
                qkv_weight[0],
                out_weight[0],
                keep_visual,
                text_saved,
                text_branch,
            )
            in_parts[1], out_parts[1], visual_query_back, text_key_back = attend_back(
                visual_rows,
                text_rows,
                qkv_weight[1],
                out_weight[1],
                keep_text,
                visual_saved,
                visual_branch,
            )
            text_part = text_query_back + text_key_back
            visual_part = visual_query_back + visual_key_back
        text_norm_grad, visual_norm_grad = (
            lax.psum_scatter(
                text_part.astype(jnp.bfloat16), "mp", scatter_dimension=0, tiled=True
            ).astype(jnp.float32),
            lax.psum_scatter(
                visual_part.astype(jnp.bfloat16), "mp", scatter_dimension=0, tiled=True
            ).astype(jnp.float32),
        )
        text_in, visual_in = inputs[sublayer]
        text_pull = jax.vjp(normalize, text_in, norm_gain[2 * sublayer], norm_shift[2 * sublayer])[
            1
        ]
        text_delta, gain_parts[2 * sublayer], shift_parts[2 * sublayer] = text_pull(text_norm_grad)
        visual_pull = jax.vjp(
            normalize, visual_in, norm_gain[2 * sublayer + 1], norm_shift[2 * sublayer + 1]
        )[1]
        visual_delta, gain_parts[2 * sublayer + 1], shift_parts[2 * sublayer + 1] = visual_pull(
            visual_norm_grad
        )
        text_back = text_back + text_delta
        visual_back = visual_back + visual_delta
    gain_grads = jnp.stack(gain_parts)
    shift_grads = jnp.stack(shift_parts)
    gain_grads, shift_grads = (
        lax.psum(gain_grads.astype(jnp.bfloat16), "mp").astype(jnp.float32),
        lax.psum(shift_grads.astype(jnp.bfloat16), "mp").astype(jnp.float32),
    )
    in_grads = jnp.stack(in_parts)
    out_grads = jnp.stack(out_parts)
    in_grads, out_grads, up_grads, down_grads, gain_grads, shift_grads = lax.psum(
        (in_grads, out_grads, up_grads, down_grads, gain_grads, shift_grads), "dp"
    )
    return (
        text_output,
        visual_output,
        text_back.astype(jnp.bfloat16),
        visual_back.astype(jnp.bfloat16),
        in_grads,
        out_grads,
        up_grads,
        down_grads,
        gain_grads,
        shift_grads,
    )


def solution(mesh):
    placed = (
        P(("dp", "mp"), None, None),
        P(("dp", "mp"), None, None),
        P("dp", None),
        P(None, None, None, "mp"),
        P(None, "mp", None),
        P(None, None, "mp"),
        P(None, "mp", None),
        P(),
        P(),
        P(("dp", "mp"), None, None),
        P(("dp", "mp"), None, None),
    )
    return jax.shard_map(
        per_device,
        mesh=mesh,
        in_specs=placed,
        out_specs=(
            P(("dp", "mp"), None, None),
            P(("dp", "mp"), None, None),
            P(("dp", "mp"), None, None),
            P(("dp", "mp"), None, None),
            P(None, None, None, "mp"),
            P(None, "mp", None),
            P(None, None, "mp"),
            P(None, "mp", None),
            P(),
            P(),
        ),
        check_vma=False,
    )
```

profile of v0, /device:TPU:0, one launch (start us, length us, event | category | flops | bytes accessed | tf_op | source)
XLA Modules:
  0.0 1437.0 jit_solution(4029345135973750773)
XLA Ops:
  20.6 18.6 %all-gather.13.cloned.1.call-done = bf16[32,40,768]{2,1,0:T(8,128)(2,1)} async-done(((bf16[8,40,768]{2,1,0:T(8,128)(2,1)}), bf16[32,40,768]{2,1,0:T(8,128)(2,1)}) %all-gather.13.cloned.1.call-update) | async-done | bytes 1966096 | tf_op jit(solution)/shard_map/all_gather | solution.py:175
  42.8 27.1 %all-gather.15.cloned.1.call-done = bf16[32,64,768]{2,1,0:T(8,128)(2,1)} async-done(((bf16[8,64,768]{2,1,0:T(8,128)(2,1)}), bf16[32,64,768]{2,1,0:T(8,128)(2,1)}) %all-gather.15.cloned.1.call-update) | async-done | bytes 3145744 | tf_op jit(solution)/shard_map/all_gather | solution.py:174
  128.9 36.9 %reduce-scatter.13.cloned.1.call-done = bf16[8,64,768]{2,1,0:T(8,128)(2,1)} async-done(((bf16[32,64,768]{2,1,0:T(8,128)(2,1)}), bf16[8,64,768]{2,1,0:T(8,128)(2,1)}) %reduce-scatter.13.cloned.1.call-update) | async-done | bytes 786448 | tf_op jit(solution)/shard_map/reduce_scatter | solution.py:199
  169.3 20.4 %all-gather.21.cloned.1.call-done = bf16[32,40,768]{2,1,0:T(8,128)(2,1)} async-done(((bf16[8,40,768]{2,1,0:T(8,128)(2,1)}), bf16[32,40,768]{2,1,0:T(8,128)(2,1)}) %all-gather.21.cloned.1.call-update) | async-done | bytes 1966096 | tf_op jit(solution)/shard_map/all_gather | solution.py:175
  257.7 37.1 %reduce-scatter.15.cloned.1.call-done = bf16[8,64,768]{2,1,0:T(8,128)(2,1)} async-done(((bf16[32,64,768]{2,1,0:T(8,128)(2,1)}), bf16[8,64,768]{2,1,0:T(8,128)(2,1)}) %reduce-scatter.15.cloned.1.call-update) | async-done | bytes 786448 | tf_op jit(solution)/shard_map/reduce_scatter | solution.py:199
  298.9 19.8 %all-gather.23.cloned.1.call-done = bf16[32,40,768]{2,1,0:T(8,128)(2,1)} async-done(((bf16[8,40,768]{2,1,0:T(8,128)(2,1)}), bf16[32,40,768]{2,1,0:T(8,128)(2,1)}) %all-gather.23.cloned.1.call-update) | async-done | bytes 1966096 | tf_op jit(solution)/shard_map/all_gather | solution.py:175
  324.3 17.8 %all-gather.31.cloned.1.call-done = bf16[32,40,768]{2,1,0:T(8,128)(2,1)} async-done(((bf16[8,40,768]{2,1,0:T(8,128)(2,1)}), bf16[32,40,768]{2,1,0:T(8,128)(2,1)}) %all-gather.31.cloned.1.call-update) | async-done | bytes 1966096 | tf_op jit(solution)/shard_map/all_gather | solution.py:222
  342.0 7.0 fusion.13
  353.8 18.9 %all-gather.19.cloned.1.call-done = bf16[32,64,768]{2,1,0:T(8,128)(2,1)} async-done(((bf16[8,64,768]{2,1,0:T(8,128)(2,1)}), bf16[32,64,768]{2,1,0:T(8,128)(2,1)}) %all-gather.19.cloned.1.call-update) | async-done | bytes 3145744 | tf_op jit(solution)/shard_map/all_gather | solution.py:174
  372.7 7.5 fusion.65
  380.3 22.4 %all-gather.25.cloned.1.call-done = bf16[32,64,768]{2,1,0:T(8,128)(2,1)} async-done(((bf16[8,64,768]{2,1,0:T(8,128)(2,1)}), bf16[32,64,768]{2,1,0:T(8,128)(2,1)}) %all-gather.25.cloned.1.call-update) | async-done | bytes 3145744 | tf_op jit(solution)/shard_map/all_gather | solution.py:221
  402.7 8.5 fusion.6
  416.9 18.7 %reduce-scatter.29.cloned.1.call-done = bf16[8,40,768]{2,1,0:T(8,128)(2,1)} async-done(((bf16[32,40,768]{2,1,0:T(8,128)(2,1)}), bf16[8,40,768]{2,1,0:T(8,128)(2,1)}) %reduce-scatter.29.cloned.1.call-update) | async-done | bytes 491536 | tf_op jit(solution)/shard_map/reduce_scatter | solution.py:275
  440.9 35.0 %reduce-scatter.25.cloned.1.call-done = bf16[8,64,768]{2,1,0:T(8,128)(2,1)} async-done(((bf16[32,64,768]{2,1,0:T(8,128)(2,1)}), bf16[8,64,768]{2,1,0:T(8,128)(2,1)}) %reduce-scatter.25.cloned.1.call-update) | async-done | bytes 786448 | tf_op jit(solution)/shard_map/reduce_scatter | solution.py:272
  480.8 19.0 %all-gather.33.cloned.1.call-done = bf16[32,40,768]{2,1,0:T(8,128)(2,1)} async-done(((bf16[8,40,768]{2,1,0:T(8,128)(2,1)}), bf16[32,40,768]{2,1,0:T(8,128)(2,1)}) %all-gather.33.cloned.1.call-update) | async-done | bytes 1966096 | tf_op jit(solution)/shard_map/all_gather | solution.py:222
  579.5 8.7 convolution_convert_fusion.1
  591.4 9.8 reduce-scatter.23.cloned.1.call-done
  617.1 24.6 %reduce-scatter.27.cloned.1.call-done = bf16[8,64,768]{2,1,0:T(8,128)(2,1)} async-done(((bf16[32,64,768]{2,1,0:T(8,128)(2,1)}), bf16[8,64,768]{2,1,0:T(8,128)(2,1)}) %reduce-scatter.27.cloned.1.call-update) | async-done | bytes 786448 | tf_op jit(solution)/shard_map/reduce_scatter | solution.py:272
  644.8 37.2 %reduce-scatter.17.cloned.1.call-done = bf16[8,64,768]{2,1,0:T(8,128)(2,1)} async-done(((bf16[32,64,768]{2,1,0:T(8,128)(2,1)}), bf16[8,64,768]{2,1,0:T(8,128)(2,1)}) %reduce-scatter.17.cloned.1.call-update) | async-done | bytes 786448 | tf_op jit(solution)/shard_map/reduce_scatter | solution.py:199
  727.7 8.9 all-gather.29.cloned.1.call-done
  771.2 8.0 convolution_bitcast_fusion
  854.7 11.2 all-reduce.2
  865.9 41.3 %all-reduce = (f32[6,768]{1,0:T(8,128)}, f32[6,768]{1,0:T(8,128)}) all-reduce(bf16[6,768]{1,0:T(8,128)(2,1)S(1)} %get-tuple-element.40, bf16[6,768]{1,0:T(8,128)(2,1)S(1)} %get-tuple-element.41), channel_id=1, replica_groups=mesh['dp'=8,'mp'=4] {'dp'}, use_global_device_ids=true, to_apply=%region_59.0 | all-reduce | flops 9216 | bytes 55296 | tf_op jit(solution)/shard_map/psum | solution.py:300
  910.1 506.4 %all-reduce.5.cloned.1.call-done = (f32[4,768,3,192]{1,3,2,0:T(8,128)}, f32[4,192,768]{2,1,0:T(8,128)}, f32[2,768,768]{2,1,0:T(8,128)}, f32[2,768,768]{2,1,0:T(8,128)}) async-done(((f32[4,768,3,192]{1,3,2,0:T(8,128)}, f32[4,192,768]{2,1,0:T(8,128)}, f32[2,768,768]{2,1,0:T(8,128)}, f32[2,768,768]{2,1,0:T(8,128)}), (f32[4,768,3,192]{1,3,2,0:T(8,128)}, f32[4,192,768]{2,1,0:T(8,128)}, f32[2,768,768]{2,1,0:T(8,128)}, ...) | async-done | bytes 18874384 | tf_op jit(solution)/shard_map/psum | solution.py:300
  (555 shorter events, 450.5 us)
Async XLA Ops:
  14.5 55.4 %all-gather.15.cloned.1.call-start = ((), (), s32[]{:S(2)}) async-start(), calls=%async_computation.13 | async-start | bytes 3932160 | tf_op jit(solution)/shard_map/all_gather | solution.py:174
  16.5 108.5 %reduce-scatter.19.cloned.1.call-start = ((), (), s32[]{:S(2)}) async-start(), calls=%async_computation.19 | async-start | bytes 2457600 | tf_op jit(solution)/shard_map/reduce_scatter | solution.py:202
  94.4 71.4 %reduce-scatter.13.cloned.1.call-start = ((), (), s32[]{:S(2)}) async-start(), calls=%async_computation.14 | async-start | bytes 3932160 | tf_op jit(solution)/shard_map/reduce_scatter | solution.py:199
  124.2 65.5 %all-gather.21.cloned.1.call-start = ((), (), s32[]{:S(2)}) async-start(), calls=%async_computation.20 | async-start | bytes 2457600 | tf_op jit(solution)/shard_map/all_gather | solution.py:175
  128.9 91.3 %all-gather.17.cloned.1.call-start = ((), (), s32[]{:S(2)}) async-start(), calls=%async_computation.15 | async-start | bytes 3932160 | tf_op jit(solution)/shard_map/all_gather | solution.py:174
  169.1 84.7 %reduce-scatter.21.cloned.1.call-start = ((), (), s32[]{:S(2)}) async-start(), calls=%async_computation.21 | async-start | bytes 2457600 | tf_op jit(solution)/shard_map/reduce_scatter | solution.py:202
  218.1 76.6 %reduce-scatter.15.cloned.1.call-start = ((), (), s32[]{:S(2)}) async-start(), calls=%async_computation.16 | async-start | bytes 3932160 | tf_op jit(solution)/shard_map/reduce_scatter | solution.py:199
  249.0 69.8 %all-gather.23.cloned.1.call-start = ((), (), s32[]{:S(2)}) async-start(), calls=%async_computation.22 | async-start | bytes 2457600 | tf_op jit(solution)/shard_map/all_gather | solution.py:175
  257.0 85.0 %all-gather.31.cloned.1.call-start = ((), (), s32[]{:S(2)}) async-start(), calls=%async_computation.29 | async-start | bytes 2457600 | tf_op jit(solution)/shard_map/all_gather | solution.py:222
  257.6 115.1 %all-gather.19.cloned.1.call-start = ((), (), s32[]{:S(2)}) async-start(), calls=%async_computation.17 | async-start | bytes 3932160 | tf_op jit(solution)/shard_map/all_gather | solution.py:174
  298.0 104.6 %all-gather.25.cloned.1.call-start = ((), (), s32[]{:S(2)}) async-start(), calls=%async_computation.24 | async-start | bytes 3932160 | tf_op jit(solution)/shard_map/all_gather | solution.py:221
  298.6 137.0 %reduce-scatter.29.cloned.1.call-start = ((), (), s32[]{:S(2)}) async-start(), calls=%async_computation.30 | async-start | bytes 2457600 | tf_op jit(solution)/shard_map/reduce_scatter | solution.py:275
  353.3 122.6 %reduce-scatter.25.cloned.1.call-start = ((), (), s32[]{:S(2)}) async-start(), calls=%async_computation.25 | async-start | bytes 3932160 | tf_op jit(solution)/shard_map/reduce_scatter | solution.py:272
  416.9 82.9 %all-gather.33.cloned.1.call-start = ((), (), s32[]{:S(2)}) async-start(), calls=%async_computation.31 | async-start | bytes 2457600 | tf_op jit(solution)/shard_map/all_gather | solution.py:222
  440.9 103.8 %all-gather.27.cloned.1.call-start = ((), (), s32[]{:S(2)}) async-start(), calls=%async_computation.26 | async-start | bytes 3932160 | tf_op jit(solution)/shard_map/all_gather | solution.py:221
  480.6 107.7 %reduce-scatter.31.cloned.1.call-start = ((), (), s32[]{:S(2)}) async-start(), calls=%async_computation.32 | async-start | bytes 2457600 | tf_op jit(solution)/shard_map/reduce_scatter | solution.py:275
  537.9 63.3 %reduce-scatter.23.cloned.1.call-start = ((), (), s32[]{:S(2)}) async-start(), calls=%async_computation.23 | async-start | bytes 2457600 | tf_op jit(solution)/shard_map/reduce_scatter | solution.py:202
  544.4 97.3 %reduce-scatter.27.cloned.1.call-start = ((), (), s32[]{:S(2)}) async-start(), calls=%async_computation.27 | async-start | bytes 3932160 | tf_op jit(solution)/shard_map/reduce_scatter | solution.py:272
  579.1 102.9 %reduce-scatter.17.cloned.1.call-start = ((), (), s32[]{:S(2)}) async-start(), calls=%async_computation.18 | async-start | bytes 3932160 | tf_op jit(solution)/shard_map/reduce_scatter | solution.py:199
  588.3 117.7 %all-gather.35.cloned.1.call-start = ((), (), s32[]{:S(2)}) async-start(), calls=%async_computation.33 | async-start | bytes 2457600 | tf_op jit(solution)/shard_map/all_gather | solution.py:222
  605.1 131.5 %all-gather.29.cloned.1.call-start = ((), (), s32[]{:S(2)}) async-start(), calls=%async_computation.28 | async-start | bytes 3932160 | tf_op jit(solution)/shard_map/all_gather | solution.py:221
  686.1 158.9 %reduce-scatter.35.cloned.1.call-start = ((), (), s32[]{:S(2)}) async-start(), calls=%async_computation.35 | async-start | bytes 2457600 | tf_op jit(solution)/shard_map/reduce_scatter | solution.py:275
  767.8 82.8 %reduce-scatter.33.cloned.1.call-start = ((), (), s32[]{:S(2)}) async-start(), calls=%async_computation.34 | async-start | bytes 3932160 | tf_op jit(solution)/shard_map/reduce_scatter | solution.py:272
  804.6 611.9 %all-reduce.5.cloned.1.call-start = ((), (), s32[]{:S(2)}) async-start(), calls=%async_computation.36 | async-start | bytes 37748736 | tf_op jit(solution)/shard_map/psum | solution.py:300
  (136 other events, 703.3 us)
Sparse Core Ops, SparseCore 0:
  14.6 24.5 all-gather.12
  41.4 28.4 all-gather.14
  94.5 30.3 reduce-scatter.18
  127.9 37.8 reduce-scatter.12
  191.6 28.4 all-gather.16
  223.3 30.3 reduce-scatter.20
  256.8 37.8 reduce-scatter.14
  296.9 21.8 all-gather.22
  320.2 21.8 all-gather.30
  344.2 28.4 all-gather.18
  374.1 28.4 all-gather.24
  405.2 30.3 reduce-scatter.28
  438.0 37.8 reduce-scatter.24
  477.9 21.8 all-gather.32
  501.8 28.4 all-gather.26
  538.0 30.3 reduce-scatter.30
  570.8 30.3 reduce-scatter.22
  603.8 37.8 reduce-scatter.26
  644.1 37.8 reduce-scatter.16
  684.1 21.8 all-gather.34
  708.1 28.4 all-gather.28
  767.9 30.3 reduce-scatter.34
  804.8 37.6 reduce-scatter.32
  847.8 568.6 all-reduce.4
  (1 shorter events, 21.8 us)
where the time goes:
time: 1450 us; the launch traced here: 1440 us
  waiting for transfers between devices  892 us (62%)
  matrix products  246 us (17%)
  local copies, waits for them, and re-layouts  150 us (10%)
  other arithmetic  77.3 us (5%)
  blocking collectives  52.5 us (4%)
  between operations  16 us (1%)
    psum x1, waiting for transfers between devices, per_device(): lax.psum((in_grads, out_grads, up_grads, down_grads, gain_grads, shift_gr...  506 us
    reduce_scatter x6, waiting for transfers between devices, per_device(): lax.psum_scatter(text_part.astype(jnp.bfloat16), 'mp', scatter_dimension=...  171 us
    dot_general x20, matrix products, linear(): jnp.einsum('pld,de->ple', activation, weight, preferred_element_type=jnp....  81.8 us
    dot_general x20, matrix products, linear_back(): jnp.einsum('ple,de->pld', gradient, weight, preferred_element_type=jnp.fl...  68.2 us
    all_gather x3, waiting for transfers between devices, per_device(): lax.all_gather(visual_norm, 'mp', axis=0, tiled=True)  58.8 us
    all_gather x3, waiting for transfers between devices, per_device(): lax.all_gather(text_norm, 'mp', axis=0, tiled=True)  47.8 us
    unnamed x274, local copies, waits for them, and re-layouts  41.7 us
    psum x1, blocking collectives, per_device(): lax.psum((in_grads, out_grads, up_grads, down_grads, gain_grads, shift_gr...  41.3 us
  transfers between devices with their start and end apart: 25, of which 21 were waited for; matrix products, arithmetic and copies ran while one was open for 26% of the time, Pallas kernels for 0%

commit v1 on v0

--- a/solution.py
+++ b/solution.py
@@ -297,9 +297,11 @@
     )
     in_grads = jnp.stack(in_parts)
     out_grads = jnp.stack(out_parts)
-    in_grads, out_grads, up_grads, down_grads, gain_grads, shift_grads = lax.psum(
-        (in_grads, out_grads, up_grads, down_grads, gain_grads, shift_grads), "dp"
-    )
+    in_grads, out_grads, up_grads, down_grads = jax.tree.map(
+        lambda grad: lax.psum(grad.astype(jnp.bfloat16), "dp").astype(jnp.float32),
+        (in_grads, out_grads, up_grads, down_grads),
+    )
+    gain_grads, shift_grads = lax.psum((gain_grads, shift_grads), "dp")
     return (
         text_output,
         visual_output,

time: 1450 us -> 1170 us (0.81)
  waiting for transfers between devices: 892 us -> 633 us
  local copies, waits for them, and re-layouts: 150 us -> 130 us
    psum x1, waiting for transfers between devices: 506 us -> 242 us  [per_device(): lax.psum(grad.astype(jnp.bfloat16), 'dp').astype(jnp.float32)]
    unnamed x274 -> x264, local copies, waits for them, and re-layouts: 41.7 us -> 27.2 us
  transfers between devices with their start and end apart: 25 -> 25, of which waited for: 21 -> 21; matrix products, arithmetic and copies ran while one was open for 26% -> 31% of each run, Pallas kernels for 0% -> 0%
where the time goes in v1:
time: 1170 us; the launch traced here: 1160 us
  waiting for transfers between devices  633 us (54%)
  matrix products  245 us (21%)
  local copies, waits for them, and re-layouts  130 us (11%)
  other arithmetic  84.9 us (7%)
  blocking collectives  51.5 us (4%)
  between operations  16 us (1%)
    psum x1, waiting for transfers between devices, per_device(): lax.psum(grad.astype(jnp.bfloat16), 'dp').astype(jnp.float32)  242 us
    reduce_scatter x6, waiting for transfers between devices, per_device(): lax.psum_scatter(text_part.astype(jnp.bfloat16), 'mp', scatter_dimension=...  171 us
    dot_general x20, matrix products, linear(): jnp.einsum('pld,de->ple', activation, weight, preferred_element_type=jnp....  82 us
    dot_general x20, matrix products, linear_back(): jnp.einsum('ple,de->pld', gradient, weight, preferred_element_type=jnp.fl...  68.1 us
    all_gather x3, waiting for transfers between devices, per_device(): lax.all_gather(visual_norm, 'mp', axis=0, tiled=True)  58.8 us
    all_gather x3, waiting for transfers between devices, per_device(): lax.all_gather(text_norm, 'mp', axis=0, tiled=True)  46.9 us
    all_gather x3, waiting for transfers between devices, per_device(): lax.all_gather(visual_back.astype(jnp.bfloat16), 'mp', axis=0, tiled=True)  42.2 us
    psum x1, blocking collectives, per_device(): gain_grads, shift_grads = lax.psum((gain_grads, shift_grads), 'dp')  40.8 us
  transfers between devices with their start and end apart: 25, of which 21 were waited for; matrix products, arithmetic and copies ran while one was open for 31% of the time, Pallas kernels for 0%

profile of v1, /device:TPU:0, one launch (start us, length us, event | category | flops | bytes accessed | tf_op | source)
XLA Modules:
  0.0 1164.2 jit_solution(13793235685979987641)
XLA Ops:
  20.7 18.6 %all-gather.13.cloned.1.call-done = bf16[32,40,768]{2,1,0:T(8,128)(2,1)} async-done(((bf16[8,40,768]{2,1,0:T(8,128)(2,1)}), bf16[32,40,768]{2,1,0:T(8,128)(2,1)}) %all-gather.13.cloned.1.call-update) | async-done | bytes 1966096 | tf_op jit(solution)/shard_map/all_gather | solution.py:175
  42.8 27.1 %all-gather.15.cloned.1.call-done = bf16[32,64,768]{2,1,0:T(8,128)(2,1)} async-done(((bf16[8,64,768]{2,1,0:T(8,128)(2,1)}), bf16[32,64,768]{2,1,0:T(8,128)(2,1)}) %all-gather.15.cloned.1.call-update) | async-done | bytes 3145744 | tf_op jit(solution)/shard_map/all_gather | solution.py:174
  127.7 37.1 %reduce-scatter.13.cloned.1.call-done = bf16[8,64,768]{2,1,0:T(8,128)(2,1)} async-done(((bf16[32,64,768]{2,1,0:T(8,128)(2,1)}), bf16[8,64,768]{2,1,0:T(8,128)(2,1)}) %reduce-scatter.13.cloned.1.call-update) | async-done | bytes 786448 | tf_op jit(solution)/shard_map/reduce_scatter | solution.py:199
  168.3 20.3 %all-gather.21.cloned.1.call-done = bf16[32,40,768]{2,1,0:T(8,128)(2,1)} async-done(((bf16[8,40,768]{2,1,0:T(8,128)(2,1)}), bf16[32,40,768]{2,1,0:T(8,128)(2,1)}) %all-gather.21.cloned.1.call-update) | async-done | bytes 1966096 | tf_op jit(solution)/shard_map/all_gather | solution.py:175
  256.6 37.1 %reduce-scatter.15.cloned.1.call-done = bf16[8,64,768]{2,1,0:T(8,128)(2,1)} async-done(((bf16[32,64,768]{2,1,0:T(8,128)(2,1)}), bf16[8,64,768]{2,1,0:T(8,128)(2,1)}) %reduce-scatter.15.cloned.1.call-update) | async-done | bytes 786448 | tf_op jit(solution)/shard_map/reduce_scatter | solution.py:199
  297.9 19.8 %all-gather.23.cloned.1.call-done = bf16[32,40,768]{2,1,0:T(8,128)(2,1)} async-done(((bf16[8,40,768]{2,1,0:T(8,128)(2,1)}), bf16[32,40,768]{2,1,0:T(8,128)(2,1)}) %all-gather.23.cloned.1.call-update) | async-done | bytes 1966096 | tf_op jit(solution)/shard_map/all_gather | solution.py:175
  323.2 17.8 %all-gather.31.cloned.1.call-done = bf16[32,40,768]{2,1,0:T(8,128)(2,1)} async-done(((bf16[8,40,768]{2,1,0:T(8,128)(2,1)}), bf16[32,40,768]{2,1,0:T(8,128)(2,1)}) %all-gather.31.cloned.1.call-update) | async-done | bytes 1966096 | tf_op jit(solution)/shard_map/all_gather | solution.py:222
  341.0 7.0 fusion.13
  352.8 18.9 %all-gather.19.cloned.1.call-done = bf16[32,64,768]{2,1,0:T(8,128)(2,1)} async-done(((bf16[8,64,768]{2,1,0:T(8,128)(2,1)}), bf16[32,64,768]{2,1,0:T(8,128)(2,1)}) %all-gather.19.cloned.1.call-update) | async-done | bytes 3145744 | tf_op jit(solution)/shard_map/all_gather | solution.py:174
  371.7 7.5 fusion.85
  379.2 22.4 %all-gather.25.cloned.1.call-done = bf16[32,64,768]{2,1,0:T(8,128)(2,1)} async-done(((bf16[8,64,768]{2,1,0:T(8,128)(2,1)}), bf16[32,64,768]{2,1,0:T(8,128)(2,1)}) %all-gather.25.cloned.1.call-update) | async-done | bytes 3145744 | tf_op jit(solution)/shard_map/all_gather | solution.py:221
  401.6 8.5 fusion.6
  415.9 18.7 %reduce-scatter.29.cloned.1.call-done = bf16[8,40,768]{2,1,0:T(8,128)(2,1)} async-done(((bf16[32,40,768]{2,1,0:T(8,128)(2,1)}), bf16[8,40,768]{2,1,0:T(8,128)(2,1)}) %reduce-scatter.29.cloned.1.call-update) | async-done | bytes 491536 | tf_op jit(solution)/shard_map/reduce_scatter | solution.py:275
  439.9 35.0 %reduce-scatter.25.cloned.1.call-done = bf16[8,64,768]{2,1,0:T(8,128)(2,1)} async-done(((bf16[32,64,768]{2,1,0:T(8,128)(2,1)}), bf16[8,64,768]{2,1,0:T(8,128)(2,1)}) %reduce-scatter.25.cloned.1.call-update) | async-done | bytes 786448 | tf_op jit(solution)/shard_map/reduce_scatter | solution.py:272
  479.8 18.9 %all-gather.33.cloned.1.call-done = bf16[32,40,768]{2,1,0:T(8,128)(2,1)} async-done(((bf16[8,40,768]{2,1,0:T(8,128)(2,1)}), bf16[32,40,768]{2,1,0:T(8,128)(2,1)}) %all-gather.33.cloned.1.call-update) | async-done | bytes 1966096 | tf_op jit(solution)/shard_map/all_gather | solution.py:222
  578.4 8.7 convolution_convert_fusion.1
  590.3 10.0 reduce-scatter.23.cloned.1.call-done
  616.1 24.6 %reduce-scatter.27.cloned.1.call-done = bf16[8,64,768]{2,1,0:T(8,128)(2,1)} async-done(((bf16[32,64,768]{2,1,0:T(8,128)(2,1)}), bf16[8,64,768]{2,1,0:T(8,128)(2,1)}) %reduce-scatter.27.cloned.1.call-update) | async-done | bytes 786448 | tf_op jit(solution)/shard_map/reduce_scatter | solution.py:272
  643.9 37.2 %reduce-scatter.17.cloned.1.call-done = bf16[8,64,768]{2,1,0:T(8,128)(2,1)} async-done(((bf16[32,64,768]{2,1,0:T(8,128)(2,1)}), bf16[8,64,768]{2,1,0:T(8,128)(2,1)}) %reduce-scatter.17.cloned.1.call-update) | async-done | bytes 786448 | tf_op jit(solution)/shard_map/reduce_scatter | solution.py:199
  726.8 9.0 all-gather.29.cloned.1.call-done
  769.6 8.5 fusion.45
  849.5 10.7 all-reduce.2
  860.3 40.8 %all-reduce = (f32[6,768]{1,0:T(8,128)}, f32[6,768]{1,0:T(8,128)}) all-reduce(bf16[6,768]{1,0:T(8,128)(2,1)S(1)} %get-tuple-element.40, bf16[6,768]{1,0:T(8,128)(2,1)S(1)} %get-tuple-element.41), channel_id=1, replica_groups=mesh['dp'=8,'mp'=4] {'dp'}, use_global_device_ids=true, to_apply=%region_59.0 | all-reduce | flops 9216 | bytes 55296 | tf_op jit(solution)/shard_map/psum | solution.py:304
  903.9 241.7 %all-reduce.5.cloned.1.call-done = (bf16[4,768,3,192]{1,3,2,0:T(8,128)(2,1)}, bf16[4,192,768]{2,1,0:T(8,128)(2,1)}, bf16[2,768,768]{2,1,0:T(8,128)(2,1)}, bf16[2,768,768]{2,1,0:T(8,128)(2,1)}) async-done(((bf16[4,768,3,192]{1,3,2,0:T(8,128)(2,1)}, bf16[4,192,768]{2,1,0:T(8,128)(2,1)}, bf16[2,768,768]{2,1,0:T(8,128)(2,1)}, bf16[2,768,768]{2,1,0:T(8,128)(2,1)}), (bf16[4,768,3,192]{1,3,2,0:T(8,128)(2,1)}, ...) | async-done | bytes 9437200 | tf_op jit(solution)/shard_map/psum | solution.py:301
  (548 shorter events, 442.2 us)
Async XLA Ops:
  14.5 55.4 %all-gather.15.cloned.1.call-start = ((), (), s32[]{:S(2)}) async-start(), calls=%async_computation.13 | async-start | bytes 3932160 | tf_op jit(solution)/shard_map/all_gather | solution.py:174
  16.5 107.4 %reduce-scatter.19.cloned.1.call-start = ((), (), s32[]{:S(2)}) async-start(), calls=%async_computation.19 | async-start | bytes 2457600 | tf_op jit(solution)/shard_map/reduce_scatter | solution.py:202
  93.3 71.4 %reduce-scatter.13.cloned.1.call-start = ((), (), s32[]{:S(2)}) async-start(), calls=%async_computation.14 | async-start | bytes 3932160 | tf_op jit(solution)/shard_map/reduce_scatter | solution.py:199
  118.2 70.4 %all-gather.21.cloned.1.call-start = ((), (), s32[]{:S(2)}) async-start(), calls=%async_computation.20 | async-start | bytes 2457600 | tf_op jit(solution)/shard_map/all_gather | solution.py:175
  127.6 91.5 %all-gather.17.cloned.1.call-start = ((), (), s32[]{:S(2)}) async-start(), calls=%async_computation.15 | async-start | bytes 3932160 | tf_op jit(solution)/shard_map/all_gather | solution.py:174
  168.0 84.7 %reduce-scatter.21.cloned.1.call-start = ((), (), s32[]{:S(2)}) async-start(), calls=%async_computation.21 | async-start | bytes 2457600 | tf_op jit(solution)/shard_map/reduce_scatter | solution.py:202
  217.9 75.8 %reduce-scatter.15.cloned.1.call-start = ((), (), s32[]{:S(2)}) async-start(), calls=%async_computation.16 | async-start | bytes 3932160 | tf_op jit(solution)/shard_map/reduce_scatter | solution.py:199
  247.9 69.8 %all-gather.23.cloned.1.call-start = ((), (), s32[]{:S(2)}) async-start(), calls=%async_computation.22 | async-start | bytes 2457600 | tf_op jit(solution)/shard_map/all_gather | solution.py:175
  255.9 85.0 %all-gather.31.cloned.1.call-start = ((), (), s32[]{:S(2)}) async-start(), calls=%async_computation.29 | async-start | bytes 2457600 | tf_op jit(solution)/shard_map/all_gather | solution.py:222
  256.5 115.1 %all-gather.19.cloned.1.call-start = ((), (), s32[]{:S(2)}) async-start(), calls=%async_computation.17 | async-start | bytes 3932160 | tf_op jit(solution)/shard_map/all_gather | solution.py:174
  297.0 104.6 %all-gather.25.cloned.1.call-start = ((), (), s32[]{:S(2)}) async-start(), calls=%async_computation.24 | async-start | bytes 3932160 | tf_op jit(solution)/shard_map/all_gather | solution.py:221
  297.6 137.0 %reduce-scatter.29.cloned.1.call-start = ((), (), s32[]{:S(2)}) async-start(), calls=%async_computation.30 | async-start | bytes 2457600 | tf_op jit(solution)/shard_map/reduce_scatter | solution.py:275
  352.3 122.6 %reduce-scatter.25.cloned.1.call-start = ((), (), s32[]{:S(2)}) async-start(), calls=%async_computation.25 | async-start | bytes 3932160 | tf_op jit(solution)/shard_map/reduce_scatter | solution.py:272
  415.9 82.9 %all-gather.33.cloned.1.call-start = ((), (), s32[]{:S(2)}) async-start(), calls=%async_computation.31 | async-start | bytes 2457600 | tf_op jit(solution)/shard_map/all_gather | solution.py:222
  439.8 103.8 %all-gather.27.cloned.1.call-start = ((), (), s32[]{:S(2)}) async-start(), calls=%async_computation.26 | async-start | bytes 3932160 | tf_op jit(solution)/shard_map/all_gather | solution.py:221
  479.6 107.6 %reduce-scatter.31.cloned.1.call-start = ((), (), s32[]{:S(2)}) async-start(), calls=%async_computation.32 | async-start | bytes 2457600 | tf_op jit(solution)/shard_map/reduce_scatter | solution.py:275
  537.0 63.3 %reduce-scatter.23.cloned.1.call-start = ((), (), s32[]{:S(2)}) async-start(), calls=%async_computation.23 | async-start | bytes 2457600 | tf_op jit(solution)/shard_map/reduce_scatter | solution.py:202
  543.3 97.4 %reduce-scatter.27.cloned.1.call-start = ((), (), s32[]{:S(2)}) async-start(), calls=%async_computation.27 | async-start | bytes 3932160 | tf_op jit(solution)/shard_map/reduce_scatter | solution.py:272
  577.9 103.1 %reduce-scatter.17.cloned.1.call-start = ((), (), s32[]{:S(2)}) async-start(), calls=%async_computation.18 | async-start | bytes 3932160 | tf_op jit(solution)/shard_map/reduce_scatter | solution.py:199
  587.1 118.0 %all-gather.35.cloned.1.call-start = ((), (), s32[]{:S(2)}) async-start(), calls=%async_computation.33 | async-start | bytes 2457600 | tf_op jit(solution)/shard_map/all_gather | solution.py:222
  604.2 131.5 %all-gather.29.cloned.1.call-start = ((), (), s32[]{:S(2)}) async-start(), calls=%async_computation.28 | async-start | bytes 3932160 | tf_op jit(solution)/shard_map/all_gather | solution.py:221
  685.2 154.6 %reduce-scatter.35.cloned.1.call-start = ((), (), s32[]{:S(2)}) async-start(), calls=%async_computation.35 | async-start | bytes 2457600 | tf_op jit(solution)/shard_map/reduce_scatter | solution.py:275
  767.0 78.4 %reduce-scatter.33.cloned.1.call-start = ((), (), s32[]{:S(2)}) async-start(), calls=%async_computation.34 | async-start | bytes 3932160 | tf_op jit(solution)/shard_map/reduce_scatter | solution.py:272
  803.4 342.2 %all-reduce.5.cloned.1.call-start = ((), (), s32[]{:S(2)}) async-start(), calls=%async_computation.36 | async-start | bytes 18874368 | tf_op jit(solution)/shard_map/psum | solution.py:301
  (133 other events, 694.3 us)
Sparse Core Ops, SparseCore 0:
  14.7 24.5 all-gather.12
  41.4 28.4 all-gather.14
  93.5 30.3 reduce-scatter.18
  126.8 37.8 reduce-scatter.12
  190.6 28.4 all-gather.16
  222.3 30.3 reduce-scatter.20
  255.8 37.8 reduce-scatter.14
  295.9 21.8 all-gather.22
  319.1 21.8 all-gather.30
  343.1 28.4 all-gather.18
  373.1 28.4 all-gather.24
  404.2 30.3 reduce-scatter.28
  437.0 37.8 reduce-scatter.24
  476.9 21.8 all-gather.32
  500.7 28.4 all-gather.26
  537.1 30.3 reduce-scatter.30
  569.9 30.3 reduce-scatter.22
  602.8 37.8 reduce-scatter.26
  643.1 37.8 reduce-scatter.16
  683.2 21.8 all-gather.34
  707.2 28.4 all-gather.28
  767.1 30.3 reduce-scatter.34
  803.5 37.8 reduce-scatter.32
  846.4 299.1 all-reduce.4
  (1 shorter events, 21.8 us)

commit v2 on v0

v2 whole, which is shorter than its diff:
```python
import jax
import jax.numpy as jnp
from jax import lax
from jax.experimental import pallas as pl
from jax.experimental.pallas import tpu as pltpu
from jax.sharding import PartitionSpec as P

HEAD = 64
EPSILON = 1e-05
CHUNKS = 2
NEG = -1e30
GELU_A = 0.7978845608028654
GELU_B = 0.044715
F32 = jnp.float32
BF16 = jnp.bfloat16


def dot_nn(a, b):
    return lax.dot_general(a, b, (((1,), (0,)), ((), ())), preferred_element_type=F32)


def dot_nt(a, b):
    return lax.dot_general(a, b, (((1,), (1,)), ((), ())), preferred_element_type=F32)


def dot_tn(a, b):
    return lax.dot_general(a, b, (((0,), (0,)), ((), ())), preferred_element_type=F32)


def head_masks(width, scale):
    lane = lax.broadcasted_iota(jnp.int32, (1, width), 1)
    return [
        jnp.where(lane // HEAD == head, scale, 0.0).astype(BF16) for head in range(width // HEAD)
    ]


def page_bias(rows, row_len, cols, col_len):
    row = lax.broadcasted_iota(jnp.int32, (rows, cols), 0) >= row_len
    col = lax.broadcasted_iota(jnp.int32, (rows, cols), 1) >= col_len
    return jnp.where(row == col, 0.0, NEG).astype(F32)


def softmax(scores):
    top = jnp.max(scores, axis=-1, keepdims=True)
    weight = jnp.exp(scores - top)
    return weight * (1.0 / jnp.sum(weight, axis=-1, keepdims=True))


def spans(tlen, vlen, pages):
    out = []
    for pair in range(pages // 2):
        text = (2 * tlen * pair, 2 * tlen, tlen)
        visual = (tlen * pages + 2 * vlen * pair, 2 * vlen, vlen)
        out.append((text, visual))
    return out


def attend_kernel(cross, tlen, vlen, pages, *refs):
    if cross:
        n_ref, w_ref, wo_ref, keep_ref, part_ref, saved_ref = refs
    else:
        n_ref, w_ref, wo_ref, part_ref, saved_ref = refs
    width = wo_ref.shape[1]
    trows = tlen * pages
    rows = trows + vlen * pages
    sides = (slice(0, trows), slice(trows, rows))
    for stream, side in enumerate(sides):
        block = n_ref[0, side, :]
        for kind in range(3):
            saved_ref[0, kind, side, :] = dot_nn(block, w_ref[stream, kind]).astype(BF16)
    scaled = head_masks(width, HEAD**-0.5)
    plain = head_masks(width, 1.0)
    for text, visual in spans(tlen, vlen, pages):
        for query, own, other in ((text, text, visual), (visual, visual, text)):
            key = other if cross else own
            bias = page_bias(query[1], query[2], key[1], key[2])
            qs = slice(query[0], query[0] + query[1])
            ks = slice(key[0], key[0] + key[1])
            q = saved_ref[0, 0, qs, :]
            k = saved_ref[0, 1, ks, :]
            v = saved_ref[0, 2, ks, :]
            context = None
            for head in range(width // HEAD):
                probs = softmax(dot_nt(q * scaled[head], k) + bias).astype(BF16)
                term = dot_nn(probs, v * plain[head])
                context = term if context is None else context + term
            if cross:
                context = context * keep_ref[0, qs, :]
            saved_ref[0, 3, qs, :] = context.astype(BF16)
    for stream, side in enumerate(sides):
        part_ref[0, side, :] = dot_nn(saved_ref[0, 3, side, :], wo_ref[stream]).astype(BF16)


def attend_back_kernel(cross, tlen, vlen, pages, *refs):
    if cross:
        n_ref, gy_ref, saved_ref, w_ref, wo_ref, keep_ref, part_ref, grad_ref, gc, d, acc = refs
    else:
        n_ref, gy_ref, saved_ref, w_ref, wo_ref, part_ref, grad_ref, gc, d, acc = refs
    step = pl.program_id(0)
    width = wo_ref.shape[1]
    trows = tlen * pages
    rows = trows + vlen * pages
    sides = (slice(0, trows), slice(trows, rows))

    @pl.when(step == 0)
    def _():
        acc[...] = jnp.zeros_like(acc)

    for stream, side in enumerate(sides):
        gy = gy_ref[0, side, :]
        grad = dot_nt(gy, wo_ref[stream]).astype(BF16)
        if cross:
            grad = grad * keep_ref[0, side, :].astype(BF16)
        gc[side, :] = grad
        at = (6 + stream) * width
        acc[at : at + width, :] += dot_tn(saved_ref[0, 3, side, :], gy)
    scaled = head_masks(width, HEAD**-0.5)
    plain = head_masks(width, 1.0)
    for text, visual in spans(tlen, vlen, pages):
        for query, own, other in ((text, text, visual), (visual, visual, text)):
            key = other if cross else own
            bias = page_bias(query[1], query[2], key[1], key[2])
            qs = slice(query[0], query[0] + query[1])
            ks = slice(key[0], key[0] + key[1])
            q = saved_ref[0, 0, qs, :]
            k = saved_ref[0, 1, ks, :]
            v = saved_ref[0, 2, ks, :]
            g = gc[qs, :]
            dq = dk = dv = 0.0
            for head in range(width // HEAD):
                q_head = q * scaled[head]
                g_head = g * plain[head]
                p = softmax(dot_nt(q_head, k) + bias)
                gp = dot_nt(g_head, v)
                gs = (p * (gp - jnp.sum(gp * p, axis=-1, keepdims=True))).astype(BF16)
                dv += dot_tn(p.astype(BF16), g_head)
                dq += dot_nn(gs, k * scaled[head])
                dk += dot_tn(gs, q_head)
            d[0, qs, :] = dq.astype(BF16)
            d[1, ks, :] = dk.astype(BF16)
            d[2, ks, :] = dv.astype(BF16)
    for stream, side in enumerate(sides):
        block = n_ref[0, side, :]
        part = None
        for kind in range(3):
            grad = d[kind, side, :]
            term = dot_nt(grad, w_ref[stream, kind])
            part = term if part is None else part + term
            at = (3 * stream + kind) * width
            acc[at : at + width, :] += dot_tn(grad, block)
        part_ref[0, side, :] = part.astype(BF16)

    @pl.when(step == pl.num_programs(0) - 1)
    def _():
        grad_ref[...] = acc[...].astype(BF16)


def feed_kernel(trows, *refs):
    n_ref, gy_ref, up_ref, down_ref, out_ref, part_ref, grad_ref, acc = refs
    step = pl.program_id(0)
    rows = n_ref.shape[1]
    depth = up_ref.shape[1]
    hid = up_ref.shape[2]

    @pl.when(step == 0)
    def _():
        acc[...] = jnp.zeros_like(acc)

    for stream, side in enumerate((slice(0, trows), slice(trows, rows))):
        block = n_ref[0, side, :]
        gy = gy_ref[0, side, :]
        pre = dot_nn(block, up_ref[stream])
        square = pre * pre
        bent = jnp.tanh(GELU_A * (pre + GELU_B * (square * pre)))
        half = 0.5 * (1.0 + bent)
        hidden = (pre * half).astype(BF16)
        slope = half + 0.5 * pre * (1.0 - bent * bent) * (GELU_A * (1.0 + 3.0 * GELU_B * square))
        out_ref[0, side, :] = dot_nn(hidden, down_ref[stream]).astype(BF16)
        g_pre = (dot_nt(gy, down_ref[stream]) * slope).astype(BF16)
        part_ref[0, side, :] = dot_nt(g_pre, up_ref[stream]).astype(BF16)
        at = stream * depth
        acc[at : at + depth, :] += dot_tn(block, g_pre)
        at = 2 * depth + stream * hid
        acc[at : at + hid, :] += dot_tn(hidden, gy)

    @pl.when(step == pl.num_programs(0) - 1)
    def _():
        grad_ref[...] = acc[...].astype(BF16)


def per_block(shape):
    return pl.BlockSpec((1,) + shape[1:], lambda i: (i,) + (0,) * (len(shape) - 1))


def whole(shape):
    return pl.BlockSpec(shape, lambda i: (0,) * len(shape))


def cost(flops, arrays):
    size = sum(a.size * a.dtype.itemsize for a in arrays)
    return pl.CostEstimate(flops=int(flops), bytes_accessed=int(size), transcendentals=0)


def attend(rows_all, weights, out_weights, keep, tlen, vlen, pages):
    blocks, rows, depth = rows_all.shape
    width = out_weights.shape[1]
    args = [rows_all, weights, out_weights]
    specs = [per_block(rows_all.shape), whole(weights.shape), whole(out_weights.shape)]
    if keep is not None:
        args.append(keep)
        specs.append(per_block(keep.shape))
    outs = (
        jax.ShapeDtypeStruct((blocks, rows, depth), BF16),
        jax.ShapeDtypeStruct((blocks, 4, rows, width), BF16),
    )

    def body(*refs):
        attend_kernel(keep is not None, tlen, vlen, pages, *refs)

    return pl.pallas_call(
        body,
        grid=(blocks,),
        in_specs=specs,
        out_specs=tuple(per_block(o.shape) for o in outs),
        out_shape=outs,
        cost_estimate=cost(2 * blocks * rows * (4 * depth * width + 1536 * width), args + list(outs)),
        name="attend_cross" if keep is not None else "attend_self",
    )(*args)


def attend_back(rows_all, grad_all, saved, weights, out_weights, keep, tlen, vlen, pages):
    blocks, rows, depth = rows_all.shape
    width = out_weights.shape[1]
    args = [rows_all, grad_all, saved, weights, out_weights]
    specs = [per_block(a.shape) for a in args[:3]] + [whole(a.shape) for a in args[3:]]
    if keep is not None:
        args.append(keep)
        specs.append(per_block(keep.shape))
    outs = (
        jax.ShapeDtypeStruct((blocks, rows, depth), BF16),
        jax.ShapeDtypeStruct((8 * width, depth), BF16),
    )

    def body(*refs):
        attend_back_kernel(keep is not None, tlen, vlen, pages, *refs)

    return pl.pallas_call(
        body,
        grid=(blocks,),
        in_specs=specs,
        out_specs=(per_block(outs[0].shape), whole(outs[1].shape)),
        out_shape=outs,
        scratch_shapes=[
            pltpu.VMEM((rows, width), BF16),
            pltpu.VMEM((3, rows, width), BF16),
            pltpu.VMEM((8 * width, depth), F32),
        ],
        cost_estimate=cost(2 * blocks * rows * (8 * depth * width + 4096 * width), args + list(outs)),
        name="attend_cross_back" if keep is not None else "attend_self_back",
    )(*args)


def feed(rows_all, grad_all, up, down, trows):
    blocks, rows, depth = rows_all.shape
    hid = up.shape[2]
    args = [rows_all, grad_all, up, down]
    outs = (
        jax.ShapeDtypeStruct((blocks, rows, depth), BF16),
        jax.ShapeDtypeStruct((blocks, rows, depth), BF16),
        jax.ShapeDtypeStruct((2 * depth + 2 * hid, depth), BF16),
    )

    def body(*refs):
        feed_kernel(trows, *refs)

    return pl.pallas_call(
        body,
        grid=(blocks,),
        in_specs=[per_block(a.shape) for a in args[:2]] + [whole(a.shape) for a in args[2:]],
        out_specs=(per_block(outs[0].shape), per_block(outs[1].shape), whole(outs[2].shape)),
        out_shape=outs,
        scratch_shapes=[pltpu.VMEM((2 * depth + 2 * hid, depth), F32)],
        cost_estimate=cost(2 * blocks * rows * 6 * depth * hid, args + list(outs)),
        name="feed_both",
    )(*args)


def swap(values, axis, bit, size):
    return lax.ppermute(values, axis, [(i, i ^ bit) for i in range(size)])


def gather_rows(values):
    pair = jnp.stack([values, swap(values, "mp", 2, 4)])
    return jnp.concatenate([pair, swap(pair, "mp", 1, 4)])


def scatter_rows(parts):
    pair = parts[:2].astype(F32) + swap(parts[2:], "mp", 1, 4).astype(F32)
    return pair[0] + swap(pair[1].astype(BF16), "mp", 2, 4).astype(F32)


def moments(values):
    center = values - jnp.mean(values, axis=-1, keepdims=True)
    spread = jnp.mean(center * center, axis=-1, keepdims=True)
    inverse = lax.rsqrt(spread + EPSILON)
    return center * inverse, inverse


def normalize(values, gain, shift):
    return (moments(values)[0] * gain + shift).astype(BF16)


def normalize_back(values, gain, grad):
    scaled, inverse = moments(values)
    inner = grad * gain
    delta = inverse * (
        inner
        - jnp.mean(inner, axis=-1, keepdims=True)
        - scaled * jnp.mean(inner * scaled, axis=-1, keepdims=True)
    )
    return delta, grad * scaled


def reduce_grads(grads, count):
    total = lax.psum(grads, "dp")
    return total.astype(F32)


def per_device(count, *arrays):
    (
        text_blocks,
        visual_blocks,
        drop_flags,
        qkv_weight,
        out_weight,
        up_weight,
        down_weight,
        norm_gain,
        norm_shift,
        text_cotangent,
        visual_cotangent,
    ) = arrays
    local, tlen, depth = text_blocks.shape
    vlen = visual_blocks.shape[1]
    width = out_weight.shape[1]
    pages = local // CHUNKS
    trows, vrows = pages * tlen, pages * vlen
    rows = trows + vrows

    def join(text, visual):
        text = text.reshape(CHUNKS, trows, depth)
        visual = visual.reshape(CHUNKS, vrows, depth)
        return [jnp.concatenate([text[c], visual[c]]) for c in range(CHUNKS)]

    def part(values):
        text = jnp.stack([v[:trows] for v in values]).reshape(local, tlen, depth)
        visual = jnp.stack([v[trows:] for v in values]).reshape(local, vlen, depth)
        return text.astype(BF16), visual.astype(BF16)

    def row_wise(pairs):
        is_text = lax.broadcasted_iota(jnp.int32, (rows, 1), 0) < trows
        return jnp.where(is_text, pairs[0], pairs[1])

    me = lax.axis_index("mp")
    order = me ^ jnp.array([0, 2, 1, 3], jnp.int32)
    keep = (1 - drop_flags).astype(F32).reshape(4, CHUNKS, pages, 2)[order]
    keep_rows = []
    for c in range(CHUNKS):
        text = jnp.repeat(keep[:, c, :, 1], tlen, axis=1)
        visual = jnp.repeat(keep[:, c, :, 0], vlen, axis=1)
        keep_rows.append(jnp.concatenate([text, visual], axis=1)[:, :, None])

    kinds = jnp.transpose(qkv_weight, (0, 2, 1, 3))
    cross_weights = jnp.stack(
        [
            jnp.stack([kinds[0, 0], kinds[1, 1], kinds[1, 2]]),
            jnp.stack([kinds[1, 0], kinds[0, 1], kinds[0, 2]]),
        ]
    )
    self_weights = kinds[2:]
    weights = (cross_weights, self_weights)
    outs = (out_weight[:2], out_weight[2:])
    gains = [row_wise((norm_gain[2 * s], norm_gain[2 * s + 1])) for s in range(3)]
    shifts = [row_wise((norm_shift[2 * s], norm_shift[2 * s + 1])) for s in range(3)]

    now = [v.astype(F32) for v in join(text_blocks, visual_blocks)]
    cotangents = join(text_cotangent, visual_cotangent)
    inputs = [list(now), None, None]
    gathered = [[None] * CHUNKS for _ in range(3)]
    saved = [[None] * CHUNKS for _ in range(2)]
    for s in range(2):
        for c in range(CHUNKS):
            gathered[s][c] = gather_rows(normalize(now[c], gains[s], shifts[s]))
            parts, saved[s][c] = attend(
                gathered[s][c],
                weights[s],
                outs[s],
                keep_rows[c] if s == 0 else None,
                tlen,
                vlen,
                pages,
            )
            now[c] = now[c] + scatter_rows(parts)
        inputs[s + 1] = list(now)
    grads_now = [v.astype(F32) for v in cotangents]
    totals = [None] * 3
    scale_sums = [None] * 3
    shift_sums = [None] * 3

    def back(s, c, parts):
        grad = scatter_rows(parts)
        delta, product = normalize_back(inputs[s][c], gains[s], grad)
        grads_now[c] = grads_now[c] + delta
        sums = [jnp.sum(v, axis=0) for v in (product[:trows], product[trows:])]
        shifts = [jnp.sum(v, axis=0) for v in (grad[:trows], grad[trows:])]
        sums, shifts = jnp.stack(sums), jnp.stack(shifts)
        scale_sums[s] = sums if scale_sums[s] is None else scale_sums[s] + sums
        shift_sums[s] = shifts if shift_sums[s] is None else shift_sums[s] + shifts

    partial = []
    for c in range(CHUNKS):
        cot = gather_rows(cotangents[c])
        rows_all = gather_rows(normalize(now[c], gains[2], shifts[2]))
        out, parts, grads = feed(rows_all, cot, up_weight, down_weight, trows)
        partial.append(grads.astype(F32))
        back(2, c, parts)
        now[c] = now[c] + scatter_rows(out)
    totals[2] = reduce_grads(sum(partial).astype(BF16), count)
    for s in (1, 0):
        partial = []
        for c in range(CHUNKS):
            grad_all = gather_rows(grads_now[c].astype(BF16))
            parts, grads = attend_back(
                gathered[s][c],
                grad_all,
                saved[s][c],
                weights[s],
                outs[s],
                keep_rows[c] if s == 0 else None,
                tlen,
                vlen,
                pages,
            )
            partial.append(grads.astype(F32))
            back(s, c, parts)
        totals[s] = reduce_grads(sum(partial).astype(BF16), count)

    small = jnp.concatenate(scale_sums + shift_sums)
    for bit in (1, 2):
        small = small + swap(small, "mp", bit, 4)
    bit = 1
    while bit < count:
        small = small + swap(small, "dp", bit, count)
        bit *= 2

    text_output, visual_output = part(now)
    text_gradient, visual_gradient = part(grads_now)
    in_parts = [t[: 6 * width].reshape(2, 3, width, depth) for t in totals[:2]]
    cross = in_parts[0]
    cross = jnp.stack(
        [
            jnp.stack([cross[0, 0], cross[1, 1], cross[1, 2]]),
            jnp.stack([cross[1, 0], cross[0, 1], cross[0, 2]]),
        ]
    )
    in_grads = jnp.transpose(jnp.concatenate([cross, in_parts[1]]), (0, 3, 1, 2))
    out_grads = jnp.concatenate([t[6 * width :].reshape(2, width, depth) for t in totals[:2]])
    hid = up_weight.shape[2]
    up_grads = totals[2][: 2 * depth].reshape(2, depth, hid)
    down_grads = totals[2][2 * depth :].reshape(2, hid, depth)
    return (
        text_output,
        visual_output,
        text_gradient,
        visual_gradient,
        in_grads,
        out_grads,
        up_grads,
        down_grads,
        small[:6],
        small[6:],
    )


def solution(mesh):
    placed = (
        P(("dp", "mp"), None, None),
        P(("dp", "mp"), None, None),
        P("dp", None),
        P(None, None, None, "mp"),
        P(None, "mp", None),
        P(None, None, "mp"),
        P(None, "mp", None),
        P(),
        P(),
        P(("dp", "mp"), None, None),
        P(("dp", "mp"), None, None),
    )
    count = mesh.shape["dp"]

    def device(*arrays):
        return per_device(count, *arrays)

    return jax.shard_map(
        device,
        mesh=mesh,
        in_specs=placed,
        out_specs=(
            P(("dp", "mp"), None, None),
            P(("dp", "mp"), None, None),
            P(("dp", "mp"), None, None),
            P(("dp", "mp"), None, None),
            P(None, None, None, "mp"),
            P(None, "mp", None),
            P(None, None, "mp"),
            P(None, "mp", None),
            P(),
            P(),
        ),
        check_vma=False,
    )
```

time: 1450 us -> 979 us (0.68)
  waiting for transfers between devices: 892 us -> 555 us
  matrix products: 246 us -> 0 us
  Pallas kernels: 0 us -> 202 us
  local copies, waits for them, and re-layouts: 150 us -> 57.7 us
  blocking collectives: 52.5 us -> 0 us
  starting transfers between devices: 4.2 us -> 43.4 us
  other arithmetic: 77.3 us -> 99.8 us
    ppermute x0 -> x53, waiting for transfers between devices: none -> 322 us  [swap(): return lax.ppermute(values, axis, [(i, i ^ bit) for i in range(size)])]
    psum x1, waiting for transfers between devices: 506 us -> 233 us  [reduce_grads(): total = lax.psum(grads, 'dp')]
    dot_general x84 -> x0, matrix products: 246 us -> none  [the longest x20 81.8 us: linear(): jnp.einsum('pld,de->ple', activation, weight, preferred_element_type=jnp....]
    reduce_scatter x12 -> x0, waiting for transfers between devices: 205 us -> none  [the longest x6 171 us: per_device(): lax.psum_scatter(text_part.astype(jnp.bfloat16), 'mp', scatter_dimension=...]
    pallas_call x0 -> x10, Pallas kernels: none -> 202 us  [the longest x4 107 us: attend_back(): pl.pallas_call(body, grid=(blocks,), in_specs=specs, out_specs=(per_block...]
    all_gather x12 -> x0, waiting for transfers between devices: 179 us -> none  [the longest x3 58.8 us: per_device(): lax.all_gather(visual_norm, 'mp', axis=0, tiled=True)]
    convert_element_type x27 -> x12, local copies, waits for them, and re-layouts: 61.1 us -> 0.78 us  [scatter_rows(): return pair[0] + swap(pair[1].astype(BF16), 'mp', 2, 4).astype(F32)]
    psum x2 -> x0, blocking collectives: 52.5 us -> none  [the longest x1 41.3 us: per_device(): lax.psum((in_grads, out_grads, up_grads, down_grads, gain_grads, shift_gr...]
  transfers between devices with their start and end apart: 25 -> 54, of which waited for: 21 -> 25; matrix products, arithmetic and copies ran while one was open for 26% -> 11% of each run, Pallas kernels for 0% -> 18%
where the time goes in v2:
time: 979 us; the launch traced here: 975 us
  waiting for transfers between devices  555 us (57%)
  Pallas kernels  202 us (21%)
  other arithmetic  99.8 us (10%)
  local copies, waits for them, and re-layouts  57.7 us (6%)
  starting transfers between devices  43.4 us (4%)
  between operations  16.3 us (2%)
    ppermute x53, waiting for transfers between devices, swap(): return lax.ppermute(values, axis, [(i, i ^ bit) for i in range(size)])  322 us
    psum x1, waiting for transfers between devices, reduce_grads(): total = lax.psum(grads, 'dp')  233 us
    pallas_call x4, Pallas kernels, attend_back(): pl.pallas_call(body, grid=(blocks,), in_specs=specs, out_specs=(per_block...  107 us
    pallas_call x4, Pallas kernels, attend(): pl.pallas_call(body, grid=(blocks,), in_specs=specs, out_specs=tuple((per...  49.7 us
    pallas_call x2, Pallas kernels, feed(): pl.pallas_call(body, grid=(blocks,), in_specs=[per_block(a.shape) for a i...  46.2 us
    ppermute x53, starting transfers between devices, swap(): return lax.ppermute(values, axis, [(i, i ^ bit) for i in range(size)])  43.3 us
    concatenate x12, other arithmetic, gather_rows(): return jnp.concatenate([pair, swap(pair, 'mp', 1, 4)])  29 us
    unnamed x193, local copies, waits for them, and re-layouts  21.1 us
  transfers between devices with their start and end apart: 54, of which 25 were waited for; matrix products, arithmetic and copies ran while one was open for 11% of the time, Pallas kernels for 18%

profile of v2, /device:TPU:0, one launch (start us, length us, event | category | flops | bytes accessed | tf_op | source)
XLA Modules:
  0.0 975.2 jit_solution(18319736694552767349)
XLA Ops:
  16.0 26.9 %collective-permute-done.14 = bf16[416,768]{1,0:T(8,128)(2,1)} collective-permute-done((bf16[416,768]{1,0:T(8,128)(2,1)}, bf16[416,768]{1,0:T(8,128)(2,1)}, u32[]{:S(2)}, u32[]{:S(2)}) %collective-permute-start.14) | collective-permute-done | bytes 639008 | tf_op jit(solution)/shard_map/ppermute | solution.py:289
  66.7 11.9 %attend_cross.3 = (bf16[4,416,768]{2,1,0:T(8,128)(2,1)}, bf16[4,4,416,192]{3,2,1,0:T(8,128)(2,1)}) custom-call(bf16[4,416,768]{2,1,0:T(8,128)(2,1)} %pad_maximum_fusion.4.refs_0_, bf16[2,3,768,192]{3,2,1,0:T(8,128)(2,1)} %pad_maximum_fusion.12.refs_1_.refs_3_, bf16[2,192,768]{2,1,0:T(8,128)(2,1)} %get-tuple-element.132.refs_2_.refs_4_, ...), custom_call_target="tpu_custom_call" | custom-call | flops 2944401408 | bytes 10033664 | tf_op jit(solution)/shard_map/attend_cross/pallas_call | solution.py:220
  104.6 14.4 %collective-permute-done.17 = bf16[416,768]{1,0:T(8,128)(2,1)S(1)} collective-permute-done((bf16[416,768]{1,0:T(8,128)(2,1)S(1)}, bf16[416,768]{1,0:T(8,128)(2,1)S(1)}, u32[]{:S(2)}, u32[]{:S(2)}) %collective-permute-start.17) | collective-permute-done | bytes 639008 | tf_op jit(solution)/shard_map/ppermute | solution.py:289
  119.6 12.6 %collective-permute-done.3 = bf16[416,768]{1,0:T(8,128)(2,1)S(1)} collective-permute-done((bf16[416,768]{1,0:T(8,128)(2,1)S(1)}, bf16[416,768]{1,0:T(8,128)(2,1)S(1)}, u32[]{:S(2)}, u32[]{:S(2)}) %collective-permute-start.3) | collective-permute-done | bytes 639008 | tf_op jit(solution)/shard_map/ppermute | solution.py:289
  135.6 15.2 %collective-permute-done.18 = bf16[416,768]{1,0:T(8,128)(2,1)S(1)} collective-permute-done((bf16[416,768]{1,0:T(8,128)(2,1)S(1)}, bf16[416,768]{1,0:T(8,128)(2,1)S(1)}, u32[]{:S(2)}, u32[]{:S(2)}) %collective-permute-start.18) | collective-permute-done | bytes 639008 | tf_op jit(solution)/shard_map/ppermute | solution.py:289
  151.0 12.2 %collective-permute-done.4 = bf16[416,768]{1,0:T(8,128)(2,1)S(1)} collective-permute-done((bf16[416,768]{1,0:T(8,128)(2,1)S(1)}, bf16[416,768]{1,0:T(8,128)(2,1)S(1)}, u32[]{:S(2)}, u32[]{:S(2)}) %collective-permute-start.4) | collective-permute-done | bytes 639008 | tf_op jit(solution)/shard_map/ppermute | solution.py:289
  167.7 13.1 %attend_self.3 = (bf16[4,416,768]{2,1,0:T(8,128)(2,1)}, bf16[4,4,416,192]{3,2,1,0:T(8,128)(2,1)}) custom-call(bf16[4,416,768]{2,1,0:T(8,128)(2,1)} %pad_maximum_fusion.5.refs_0_, bf16[2,3,768,192]{3,2,1,0:T(8,128)(2,1)} %slice.548.refs_1_.refs_3_, bf16[2,192,768]{2,1,0:T(8,128)(2,1)} %get-tuple-element.131.refs_2_.refs_4_), custom_call_target="tpu_custom_call" | custom-call | flops 2944401408 | bytes 10027008 | tf_op jit(solution)/shard_map/attend_self/pallas_call | solution.py:220
  186.9 12.9 %attend_self.2 = (bf16[4,416,768]{2,1,0:T(8,128)(2,1)}, bf16[4,4,416,192]{3,2,1,0:T(8,128)(2,1)}) custom-call(bf16[4,416,768]{2,1,0:T(8,128)(2,1)} %pad_maximum_fusion.1.refs_0_, bf16[2,3,768,192]{3,2,1,0:T(8,128)(2,1)} %slice.548.refs_1_.refs_3_, bf16[2,192,768]{2,1,0:T(8,128)(2,1)} %get-tuple-element.131.refs_2_.refs_4_), custom_call_target="tpu_custom_call" | custom-call | flops 2944401408 | bytes 10027008 | tf_op jit(solution)/shard_map/attend_self/pallas_call | solution.py:220
  209.8 23.4 %collective-permute-done.21 = bf16[416,768]{1,0:T(8,128)(2,1)S(1)} collective-permute-done((bf16[416,768]{1,0:T(8,128)(2,1)S(1)}, bf16[416,768]{1,0:T(8,128)(2,1)S(1)}, u32[]{:S(2)}, u32[]{:S(2)}) %collective-permute-start.21) | collective-permute-done | bytes 639008 | tf_op jit(solution)/shard_map/ppermute | solution.py:289
  233.8 26.1 %collective-permute-done.7 = bf16[416,768]{1,0:T(8,128)(2,1)S(1)} collective-permute-done((bf16[416,768]{1,0:T(8,128)(2,1)S(1)}, bf16[416,768]{1,0:T(8,128)(2,1)S(1)}, u32[]{:S(2)}, u32[]{:S(2)}) %collective-permute-start.7) | collective-permute-done | bytes 639008 | tf_op jit(solution)/shard_map/ppermute | solution.py:289
  264.0 13.1 %collective-permute-done.22 = bf16[416,768]{1,0:T(8,128)(2,1)S(1)} collective-permute-done((bf16[416,768]{1,0:T(8,128)(2,1)S(1)}, bf16[416,768]{1,0:T(8,128)(2,1)S(1)}, u32[]{:S(2)}, u32[]{:S(2)}) %collective-permute-start.22) | collective-permute-done | bytes 639008 | tf_op jit(solution)/shard_map/ppermute | solution.py:289
  297.1 23.3 %feed_both.3 = (bf16[4,416,768]{2,1,0:T(8,128)(2,1)}, bf16[4,416,768]{2,1,0:T(8,128)(2,1)}, bf16[3072,768]{1,0:T(8,128)(2,1)}) custom-call(bf16[4,416,768]{2,1,0:T(8,128)(2,1)} %pad_maximum_fusion.6.refs_0_, bf16[4,416,768]{2,1,0:T(8,128)(2,1)} %pad_maximum_fusion.7.refs_1_, bf16[2,768,768]{2,1,0:T(8,128)(2,1)} %refs_2_.3, bf16[2,768,768]{2,1,0:T(8,128)(2,1)} %refs_3_.3), custom_call_target="tpu_custom_call" | custom-call | flops 11777605632 | bytes 19660800 | tf_op jit(solution)/shard_map/feed_both/pallas_call | solution.py:276
  327.8 22.9 %feed_both.2 = (bf16[4,416,768]{2,1,0:T(8,128)(2,1)}, bf16[4,416,768]{2,1,0:T(8,128)(2,1)}, bf16[3072,768]{1,0:T(8,128)(2,1)}) custom-call(bf16[4,416,768]{2,1,0:T(8,128)(2,1)} %pad_maximum_fusion.2.refs_0_, bf16[4,416,768]{2,1,0:T(8,128)(2,1)} %pad_maximum_fusion.3.refs_1_, bf16[2,768,768]{2,1,0:T(8,128)(2,1)} %refs_2_.3, bf16[2,768,768]{2,1,0:T(8,128)(2,1)} %refs_3_.3), custom_call_target="tpu_custom_call" | custom-call | flops 11777605632 | bytes 19660800 | tf_op jit(solution)/shard_map/feed_both/pallas_call | solution.py:276
  375.1 25.5 %collective-permute-done.29 = bf16[416,768]{1,0:T(8,128)(2,1)S(1)} collective-permute-done((bf16[416,768]{1,0:T(8,128)(2,1)S(1)}, bf16[416,768]{1,0:T(8,128)(2,1)S(1)}, u32[]{:S(2)}, u32[]{:S(2)}) %collective-permute-start.29) | collective-permute-done | bytes 639008 | tf_op jit(solution)/shard_map/ppermute | solution.py:289
  407.5 15.1 %collective-permute-done.40 = bf16[416,768]{1,0:T(8,128)(2,1)S(1)} collective-permute-done((bf16[416,768]{1,0:T(8,128)(2,1)S(1)}, bf16[416,768]{1,0:T(8,128)(2,1)S(1)}, u32[]{:S(2)}, u32[]{:S(2)}) %collective-permute-start.40) | collective-permute-done | bytes 639008 | tf_op jit(solution)/shard_map/ppermute | solution.py:289
  422.8 12.1 %collective-permute-done.13 = bf16[416,768]{1,0:T(8,128)(2,1)S(1)} collective-permute-done((bf16[416,768]{1,0:T(8,128)(2,1)S(1)}, bf16[416,768]{1,0:T(8,128)(2,1)S(1)}, u32[]{:S(2)}, u32[]{:S(2)}) %collective-permute-start.13) | collective-permute-done | bytes 639008 | tf_op jit(solution)/shard_map/ppermute | solution.py:289
  438.7 13.3 %collective-permute-done.30 = bf16[416,768]{1,0:T(8,128)(2,1)S(1)} collective-permute-done((bf16[416,768]{1,0:T(8,128)(2,1)S(1)}, bf16[416,768]{1,0:T(8,128)(2,1)S(1)}, u32[]{:S(2)}, u32[]{:S(2)}) %collective-permute-start.30) | collective-permute-done | bytes 639008 | tf_op jit(solution)/shard_map/ppermute | solution.py:289
  455.1 26.3 %attend_self_back.3 = (bf16[4,416,768]{2,1,0:T(8,128)(2,1)}, bf16[1536,768]{1,0:T(8,128)(2,1)}) custom-call(bf16[4,416,768]{2,1,0:T(8,128)(2,1)} %pad_maximum_fusion.5.refs_0_, bf16[4,416,768]{2,1,0:T(8,128)(2,1)} %pad_maximum_fusion.10.refs_1_, bf16[4,4,416,192]{3,2,1,0:T(8,128)(2,1)} %get-tuple-element.44.refs_2_, ...), custom_call_target="tpu_custom_call" | custom-call | flops 6543114240 | bytes 14942208 | tf_op jit(solution)/shard_map/attend_self_back/pallas_call | solution.py:247
  487.6 26.2 %attend_self_back.2 = (bf16[4,416,768]{2,1,0:T(8,128)(2,1)}, bf16[1536,768]{1,0:T(8,128)(2,1)}) custom-call(bf16[4,416,768]{2,1,0:T(8,128)(2,1)} %pad_maximum_fusion.1.refs_0_, bf16[4,416,768]{2,1,0:T(8,128)(2,1)} %pad_maximum_fusion.8.refs_1_, bf16[4,4,416,192]{3,2,1,0:T(8,128)(2,1)} %get-tuple-element.39.refs_2_, ...), custom_call_target="tpu_custom_call" | custom-call | flops 6543114240 | bytes 14942208 | tf_op jit(solution)/shard_map/attend_self_back/pallas_call | solution.py:247
  520.5 14.5 %collective-permute-done.43 = bf16[416,768]{1,0:T(8,128)(2,1)S(1)} collective-permute-done((bf16[416,768]{1,0:T(8,128)(2,1)S(1)}, bf16[416,768]{1,0:T(8,128)(2,1)S(1)}, u32[]{:S(2)}, u32[]{:S(2)}) %collective-permute-start.43) | collective-permute-done | bytes 639008 | tf_op jit(solution)/shard_map/ppermute | solution.py:289
  588.9 26.9 %attend_cross_back.2 = (bf16[4,416,768]{2,1,0:T(8,128)(2,1)}, bf16[1536,768]{1,0:T(8,128)(2,1)}) custom-call(bf16[4,416,768]{2,1,0:T(8,128)(2,1)} %pad_maximum_fusion.refs_0_, bf16[4,416,768]{2,1,0:T(8,128)(2,1)} %pad_maximum_fusion.9.refs_1_, bf16[4,4,416,192]{3,2,1,0:T(8,128)(2,1)} %get-tuple-element.41.refs_2_, ...), custom_call_target="tpu_custom_call" | custom-call | flops 6543114240 | bytes 14948864 | tf_op jit(solution)/shard_map/attend_cross_back/pallas_call | solution.py:247
  618.8 27.1 %attend_cross_back.3 = (bf16[4,416,768]{2,1,0:T(8,128)(2,1)}, bf16[1536,768]{1,0:T(8,128)(2,1)}) custom-call(bf16[4,416,768]{2,1,0:T(8,128)(2,1)} %pad_maximum_fusion.4.refs_0_, bf16[4,416,768]{2,1,0:T(8,128)(2,1)} %pad_maximum_fusion.11.refs_1_, bf16[4,4,416,192]{3,2,1,0:T(8,128)(2,1)} %get-tuple-element.46.refs_2_, ...), custom_call_target="tpu_custom_call" | custom-call | flops 6543114240 | bytes 14948864 | tf_op jit(solution)/shard_map/attend_cross_back/pallas_call | solution.py:247
  661.4 13.9 %collective-permute-done.37 = bf16[416,768]{1,0:T(8,128)(2,1)S(1)} collective-permute-done((bf16[416,768]{1,0:T(8,128)(2,1)S(1)}, bf16[416,768]{1,0:T(8,128)(2,1)S(1)}, u32[]{:S(2)}, u32[]{:S(2)}) %collective-permute-start.37) | collective-permute-done | bytes 639008 | tf_op jit(solution)/shard_map/ppermute | solution.py:289
  718.8 233.1 %all-reduce.3.cloned.1.call-done = (bf16[1536,768]{1,0:T(8,128)(2,1)}, bf16[1536,768]{1,0:T(8,128)(2,1)}, bf16[3072,768]{1,0:T(8,128)(2,1)}) async-done(((bf16[1536,768]{1,0:T(8,128)(2,1)}, bf16[1536,768]{1,0:T(8,128)(2,1)}, bf16[3072,768]{1,0:T(8,128)(2,1)}), (bf16[1536,768]{1,0:T(8,128)(2,1)}, bf16[1536,768]{1,0:T(8,128)(2,1)}, bf16[3072,768]{1,0:T(8,128)(2,1)})) %all-reduce.3.cloned.1.call-update) | async-done | bytes 9437200 | tf_op jit(solution)/shard_map/psum | solution.py:325
  (521 shorter events, 296.6 us)
Async XLA Ops:
  7.2 944.8 %all-reduce.3.cloned.1.call-start = ((), (), s32[]{:S(2)}) async-start(), calls=%async_computation | async-start | bytes 18874368 | tf_op jit(solution)/shard_map/psum | solution.py:325
  11.5 43.1 %collective-permute-start = (bf16[416,768]{1,0:T(8,128)(2,1)}, bf16[416,768]{1,0:T(8,128)(2,1)}, u32[]{:S(2)}, u32[]{:S(2)}) collective-permute-start(bf16[416,768]{1,0:T(8,128)(2,1)} %get-tuple-element.153), channel_id=1, source_target_pairs={{0,2},{1,3},{2,0},{3,1},{4,6},{5,7},{6,4},{7,5},{8,10},{9,11},{10,... | collective-permute-start | bytes 1916936 | tf_op jit(solution)/shard_map/ppermute | solution.py:289
  14.5 28.4 %collective-permute-start.14 = (bf16[416,768]{1,0:T(8,128)(2,1)}, bf16[416,768]{1,0:T(8,128)(2,1)}, u32[]{:S(2)}, u32[]{:S(2)}) collective-permute-start(bf16[416,768]{1,0:T(8,128)(2,1)} %get-tuple-element.154), channel_id=1, source_target_pairs={{0,2},{1,3},{2,0},{3,1},{4,6},{5,7},{6,4},{7,5},{8,10},{9,11},{10,... | collective-permute-start | bytes 1916936 | tf_op jit(solution)/shard_map/ppermute | solution.py:289
  56.9 25.8 %collective-permute-start.1 = (bf16[2,416,768]{2,1,0:T(8,128)(2,1)}, bf16[2,416,768]{2,1,0:T(8,128)(2,1)}, u32[]{:S(2)}, u32[]{:S(2)}) collective-permute-start(bf16[2,416,768]{2,1,0:T(8,128)(2,1)} %pad_maximum_fusion.14), channel_id=1, source_target_pairs={{0,1},{1,0},{2,3},{3,2},{4,5},{5,4},{6,7},{7,6},{8,9},{9,8},{10,11... | collective-permute-start | bytes 3833864 | tf_op jit(solution)/shard_map/ppermute | solution.py:289
  103.8 28.4 %collective-permute-start.3 = (bf16[416,768]{1,0:T(8,128)(2,1)S(1)}, bf16[416,768]{1,0:T(8,128)(2,1)S(1)}, u32[]{:S(2)}, u32[]{:S(2)}) collective-permute-start(bf16[416,768]{1,0:T(8,128)(2,1)S(1)} %fusion.58), channel_id=1, source_target_pairs={{0,2},{1,3},{2,0},{3,1},{4,6},{5,7},{6,4},{7,5},{8,10},{9,11},{10,... | collective-permute-start | bytes 1916936 | tf_op jit(solution)/shard_map/ppermute | solution.py:289
  135.3 27.9 %collective-permute-start.4 = (bf16[416,768]{1,0:T(8,128)(2,1)S(1)}, bf16[416,768]{1,0:T(8,128)(2,1)S(1)}, u32[]{:S(2)}, u32[]{:S(2)}) collective-permute-start(bf16[416,768]{1,0:T(8,128)(2,1)S(1)} %get-tuple-element.149), channel_id=1, source_target_pairs={{0,2},{1,3},{2,0},{3,1},{4,6},{5,7},{6,4},{7,5},{8,10},{9,11},{10,... | collective-permute-start | bytes 1916936 | tf_op jit(solution)/shard_map/ppermute | solution.py:289
  183.4 20.7 %collective-permute-start.20 = (bf16[2,416,768]{2,1,0:T(8,128)(2,1)}, bf16[2,416,768]{2,1,0:T(8,128)(2,1)}, u32[]{:S(2)}, u32[]{:S(2)}) collective-permute-start(bf16[2,416,768]{2,1,0:T(8,128)(2,1)} %slice.458), channel_id=1, source_target_pairs={{0,1},{1,0},{2,3},{3,2},{4,5},{5,4},{6,7},{7,6},{8,9},{9,8},{10,11... | collective-permute-start | bytes 3833864 | tf_op jit(solution)/shard_map/ppermute | solution.py:289
  202.3 61.0 %collective-permute-start.24 = (bf16[416,768]{1,0:T(8,128)(2,1)S(1)}, bf16[416,768]{1,0:T(8,128)(2,1)S(1)}, u32[]{:S(2)}, u32[]{:S(2)}) collective-permute-start(bf16[416,768]{1,0:T(8,128)(2,1)S(1)} %get-tuple-element.140), channel_id=1, source_target_pairs={{0,2},{1,3},{2,0},{3,1},{4,6},{5,7},{6,4},{7,5},{8,10},{9,11},{10,... | collective-permute-start | bytes 1916936 | tf_op jit(solution)/shard_map/ppermute | solution.py:289
  205.7 27.5 %collective-permute-start.21 = (bf16[416,768]{1,0:T(8,128)(2,1)S(1)}, bf16[416,768]{1,0:T(8,128)(2,1)S(1)}, u32[]{:S(2)}, u32[]{:S(2)}) collective-permute-start(bf16[416,768]{1,0:T(8,128)(2,1)S(1)} %fusion.62), channel_id=1, source_target_pairs={{0,2},{1,3},{2,0},{3,1},{4,6},{5,7},{6,4},{7,5},{8,10},{9,11},{10,... | collective-permute-start | bytes 1916936 | tf_op jit(solution)/shard_map/ppermute | solution.py:289
  207.2 55.8 %collective-permute-start.10 = (bf16[416,768]{1,0:T(8,128)(2,1)S(1)}, bf16[416,768]{1,0:T(8,128)(2,1)S(1)}, u32[]{:S(2)}, u32[]{:S(2)}) collective-permute-start(bf16[416,768]{1,0:T(8,128)(2,1)S(1)} %get-tuple-element.138), channel_id=1, source_target_pairs={{0,2},{1,3},{2,0},{3,1},{4,6},{5,7},{6,4},{7,5},{8,10},{9,11},{10,... | collective-permute-start | bytes 1916936 | tf_op jit(solution)/shard_map/ppermute | solution.py:289
  208.4 51.6 %collective-permute-start.7 = (bf16[416,768]{1,0:T(8,128)(2,1)S(1)}, bf16[416,768]{1,0:T(8,128)(2,1)S(1)}, u32[]{:S(2)}, u32[]{:S(2)}) collective-permute-start(bf16[416,768]{1,0:T(8,128)(2,1)S(1)} %fusion.59), channel_id=1, source_target_pairs={{0,2},{1,3},{2,0},{3,1},{4,6},{5,7},{6,4},{7,5},{8,10},{9,11},{10,... | collective-permute-start | bytes 1916936 | tf_op jit(solution)/shard_map/ppermute | solution.py:289
  295.3 29.4 %collective-permute-start.9 = (bf16[2,416,768]{2,1,0:T(8,128)(2,1)}, bf16[2,416,768]{2,1,0:T(8,128)(2,1)}, u32[]{:S(2)}, u32[]{:S(2)}) collective-permute-start(bf16[2,416,768]{2,1,0:T(8,128)(2,1)} %pad_maximum_fusion.16), channel_id=1, source_target_pairs={{0,1},{1,0},{2,3},{3,2},{4,5},{5,4},{6,7},{7,6},{8,9},{9,8},{10,11... | collective-permute-start | bytes 3833864 | tf_op jit(solution)/shard_map/ppermute | solution.py:289
  324.2 29.3 %collective-permute-start.38 = (bf16[2,416,768]{2,1,0:T(8,128)(2,1)}, bf16[2,416,768]{2,1,0:T(8,128)(2,1)}, u32[]{:S(2)}, u32[]{:S(2)}) collective-permute-start(bf16[2,416,768]{2,1,0:T(8,128)(2,1)} %slice.484), channel_id=1, source_target_pairs={{0,1},{1,0},{2,3},{3,2},{4,5},{5,4},{6,7},{7,6},{8,9},{9,8},{10,11... | collective-permute-start | bytes 3833864 | tf_op jit(solution)/shard_map/ppermute | solution.py:289
  324.7 33.4 %collective-permute-start.26 = (bf16[2,416,768]{2,1,0:T(8,128)(2,1)}, bf16[2,416,768]{2,1,0:T(8,128)(2,1)}, u32[]{:S(2)}, u32[]{:S(2)}) collective-permute-start(bf16[2,416,768]{2,1,0:T(8,128)(2,1)} %slice.464), channel_id=1, source_target_pairs={{0,1},{1,0},{2,3},{3,2},{4,5},{5,4},{6,7},{7,6},{8,9},{9,8},{10,11... | collective-permute-start | bytes 3833864 | tf_op jit(solution)/shard_map/ppermute | solution.py:289
  360.0 42.9 %collective-permute-start.27 = (bf16[416,768]{1,0:T(8,128)(2,1)S(1)}, bf16[416,768]{1,0:T(8,128)(2,1)S(1)}, u32[]{:S(2)}, u32[]{:S(2)}) collective-permute-start(bf16[416,768]{1,0:T(8,128)(2,1)S(1)} %fusion.63), channel_id=1, source_target_pairs={{0,2},{1,3},{2,0},{3,1},{4,6},{5,7},{6,4},{7,5},{8,10},{9,11},{10,... | collective-permute-start | bytes 1916936 | tf_op jit(solution)/shard_map/ppermute | solution.py:289
  360.8 39.8 %collective-permute-start.29 = (bf16[416,768]{1,0:T(8,128)(2,1)S(1)}, bf16[416,768]{1,0:T(8,128)(2,1)S(1)}, u32[]{:S(2)}, u32[]{:S(2)}) collective-permute-start(bf16[416,768]{1,0:T(8,128)(2,1)S(1)} %fusion.64), channel_id=1, source_target_pairs={{0,2},{1,3},{2,0},{3,1},{4,6},{5,7},{6,4},{7,5},{8,10},{9,11},{10,... | collective-permute-start | bytes 1916936 | tf_op jit(solution)/shard_map/ppermute | solution.py:289
  407.1 27.8 %collective-permute-start.13 = (bf16[416,768]{1,0:T(8,128)(2,1)S(1)}, bf16[416,768]{1,0:T(8,128)(2,1)S(1)}, u32[]{:S(2)}, u32[]{:S(2)}) collective-permute-start(bf16[416,768]{1,0:T(8,128)(2,1)S(1)} %fusion.60), channel_id=1, source_target_pairs={{0,2},{1,3},{2,0},{3,1},{4,6},{5,7},{6,4},{7,5},{8,10},{9,11},{10,... | collective-permute-start | bytes 1916936 | tf_op jit(solution)/shard_map/ppermute | solution.py:289
  422.7 30.6 %collective-permute-start.41 = (bf16[2,416,768]{2,1,0:T(8,128)(2,1)S(1)}, bf16[2,416,768]{2,1,0:T(8,128)(2,1)S(1)}, u32[]{:S(2)}, u32[]{:S(2)}) collective-permute-start(bf16[2,416,768]{2,1,0:T(8,128)(2,1)S(1)} %pad_maximum_fusion.24), channel_id=1, source_target_pairs={{0,1},{1,0},{2,3},{3,2},{4,5},{5,4},{6,7},{7,6},{8,9},{9,8},{10,11... | collective-permute-start | bytes 3833864 | tf_op jit(solution)/shard_map/ppermute | solution.py:289
  453.3 31.2 %collective-permute-start.31 = (bf16[2,416,768]{2,1,0:T(8,128)(2,1)}, bf16[2,416,768]{2,1,0:T(8,128)(2,1)}, u32[]{:S(2)}, u32[]{:S(2)}) collective-permute-start(bf16[2,416,768]{2,1,0:T(8,128)(2,1)} %pad_maximum_fusion.22), channel_id=1, source_target_pairs={{0,1},{1,0},{2,3},{3,2},{4,5},{5,4},{6,7},{7,6},{8,9},{9,8},{10,11... | collective-permute-start | bytes 3833864 | tf_op jit(solution)/shard_map/ppermute | solution.py:289
  483.9 31.4 %collective-permute-start.42 = (bf16[2,416,768]{2,1,0:T(8,128)(2,1)}, bf16[2,416,768]{2,1,0:T(8,128)(2,1)}, u32[]{:S(2)}, u32[]{:S(2)}) collective-permute-start(bf16[2,416,768]{2,1,0:T(8,128)(2,1)} %slice.488), channel_id=1, source_target_pairs={{0,1},{1,0},{2,3},{3,2},{4,5},{5,4},{6,7},{7,6},{8,9},{9,8},{10,11... | collective-permute-start | bytes 3833864 | tf_op jit(solution)/shard_map/ppermute | solution.py:289
  519.8 27.9 %collective-permute-start.33 = (bf16[416,768]{1,0:T(8,128)(2,1)S(1)}, bf16[416,768]{1,0:T(8,128)(2,1)S(1)}, u32[]{:S(2)}, u32[]{:S(2)}) collective-permute-start(bf16[416,768]{1,0:T(8,128)(2,1)S(1)} %fusion.65), channel_id=1, source_target_pairs={{0,2},{1,3},{2,0},{3,1},{4,6},{5,7},{6,4},{7,5},{8,10},{9,11},{10,... | collective-permute-start | bytes 1916936 | tf_op jit(solution)/shard_map/ppermute | solution.py:289
  559.2 23.6 %collective-permute-start.44 = (bf16[416,768]{1,0:T(8,128)(2,1)S(1)}, bf16[416,768]{1,0:T(8,128)(2,1)S(1)}, u32[]{:S(2)}, u32[]{:S(2)}) collective-permute-start(bf16[416,768]{1,0:T(8,128)(2,1)S(1)} %get-tuple-element.157), channel_id=1, source_target_pairs={{0,2},{1,3},{2,0},{3,1},{4,6},{5,7},{6,4},{7,5},{8,10},{9,11},{10,... | collective-permute-start | bytes 1916936 | tf_op jit(solution)/shard_map/ppermute | solution.py:289
  584.0 31.7 %collective-permute-start.45 = (bf16[2,416,768]{2,1,0:T(8,128)(2,1)}, bf16[2,416,768]{2,1,0:T(8,128)(2,1)}, u32[]{:S(2)}, u32[]{:S(2)}) collective-permute-start(bf16[2,416,768]{2,1,0:T(8,128)(2,1)} %pad_maximum_fusion.25), channel_id=1, source_target_pairs={{0,1},{1,0},{2,3},{3,2},{4,5},{5,4},{6,7},{7,6},{8,9},{9,8},{10,11... | collective-permute-start | bytes 3833864 | tf_op jit(solution)/shard_map/ppermute | solution.py:289
  660.1 27.5 %collective-permute-start.47 = (bf16[416,768]{1,0:T(8,128)(2,1)S(1)}, bf16[416,768]{1,0:T(8,128)(2,1)S(1)}, u32[]{:S(2)}, u32[]{:S(2)}) collective-permute-start(bf16[416,768]{1,0:T(8,128)(2,1)S(1)} %fusion.69), channel_id=1, source_target_pairs={{0,2},{1,3},{2,0},{3,1},{4,6},{5,7},{6,4},{7,5},{8,10},{9,11},{10,... | collective-permute-start | bytes 1916936 | tf_op jit(solution)/shard_map/ppermute | solution.py:289
  (126 other events, 1199.2 us)
Sparse Core Ops, SparseCore 0:
  650.5 301.4 all-reduce.2

commit v3 on v2

--- a/solution.py
+++ b/solution.py
@@ -55,17 +55,36 @@
     return out
 
 
+def pick(step, refs, block):
+    for at, ref in enumerate(refs):
+
+        @pl.when(step == at)
+        def _():
+            block[...] = ref[...]
+
+
+def place(step, refs, block):
+    for at, ref in enumerate(refs):
+
+        @pl.when(step == at)
+        def _():
+            ref[...] = block[...]
+
+
 def attend_kernel(cross, tlen, vlen, pages, *refs):
+    n_refs, refs = refs[:4], refs[4:]
     if cross:
-        n_ref, w_ref, wo_ref, keep_ref, part_ref, saved_ref = refs
+        w_ref, wo_ref, keep_ref, *part_refs, saved_ref, n, part = refs
     else:
-        n_ref, w_ref, wo_ref, part_ref, saved_ref = refs
+        w_ref, wo_ref, *part_refs, saved_ref, n, part = refs
+    step = pl.program_id(0)
+    pick(step, n_refs, n)
     width = wo_ref.shape[1]
     trows = tlen * pages
     rows = trows + vlen * pages
     sides = (slice(0, trows), slice(trows, rows))
     for stream, side in enumerate(sides):
-        block = n_ref[0, side, :]
+        block = n[side, :]
         for kind in range(3):
             saved_ref[0, kind, side, :] = dot_nn(block, w_ref[stream, kind]).astype(BF16)
     scaled = head_masks(width, HEAD**-0.5)
@@ -88,15 +107,19 @@
                 context = context * keep_ref[0, qs, :]
             saved_ref[0, 3, qs, :] = context.astype(BF16)
     for stream, side in enumerate(sides):
-        part_ref[0, side, :] = dot_nn(saved_ref[0, 3, side, :], wo_ref[stream]).astype(BF16)
+        part[side, :] = dot_nn(saved_ref[0, 3, side, :], wo_ref[stream]).astype(BF16)
+    place(step, part_refs, part)
 
 
 def attend_back_kernel(cross, tlen, vlen, pages, *refs):
+    n_refs, gy_refs, refs = refs[:4], refs[4:8], refs[8:]
     if cross:
-        n_ref, gy_ref, saved_ref, w_ref, wo_ref, keep_ref, part_ref, grad_ref, gc, d, acc = refs
+        saved_ref, w_ref, wo_ref, keep_ref, *part_refs, grad_ref, n, gy_all, gc, d, acc = refs
     else:
-        n_ref, gy_ref, saved_ref, w_ref, wo_ref, part_ref, grad_ref, gc, d, acc = refs
+        saved_ref, w_ref, wo_ref, *part_refs, grad_ref, n, gy_all, gc, d, acc = refs
     step = pl.program_id(0)
+    pick(step, n_refs, n)
+    pick(step, gy_refs, gy_all)
     width = wo_ref.shape[1]
     trows = tlen * pages
     rows = trows + vlen * pages
@@ -107,7 +130,7 @@
         acc[...] = jnp.zeros_like(acc)
 
     for stream, side in enumerate(sides):
-        gy = gy_ref[0, side, :]
+        gy = gy_all[side, :]
         grad = dot_nt(gy, wo_ref[stream]).astype(BF16)
         if cross:
             grad = grad * keep_ref[0, side, :].astype(BF16)
@@ -140,7 +163,7 @@
             d[1, ks, :] = dk.astype(BF16)
             d[2, ks, :] = dv.astype(BF16)
     for stream, side in enumerate(sides):
-        block = n_ref[0, side, :]
+        block = n[side, :]
         part = None
         for kind in range(3):
             grad = d[kind, side, :]
@@ -148,7 +171,8 @@
             part = term if part is None else part + term
             at = (3 * stream + kind) * width
             acc[at : at + width, :] += dot_tn(grad, block)
-        part_ref[0, side, :] = part.astype(BF16)
+        gy_all[side, :] = part.astype(BF16)
+    place(step, part_refs, gy_all)
 
     @pl.when(step == pl.num_programs(0) - 1)
     def _():
@@ -156,9 +180,14 @@
 
 
 def feed_kernel(trows, *refs):
-    n_ref, gy_ref, up_ref, down_ref, out_ref, part_ref, grad_ref, acc = refs
+    n_refs, gy_refs, refs = refs[:4], refs[4:8], refs[8:]
+    up_ref, down_ref, refs = refs[0], refs[1], refs[2:]
+    out_refs, part_refs, refs = refs[:4], refs[4:8], refs[8:]
+    grad_ref, n, gy_all, out, part, acc = refs
     step = pl.program_id(0)
-    rows = n_ref.shape[1]
+    pick(step, n_refs, n)
+    pick(step, gy_refs, gy_all)
+    rows = n.shape[0]
     depth = up_ref.shape[1]
     hid = up_ref.shape[2]
 
@@ -167,21 +196,23 @@
         acc[...] = jnp.zeros_like(acc)
 
     for stream, side in enumerate((slice(0, trows), slice(trows, rows))):
-        block = n_ref[0, side, :]
-        gy = gy_ref[0, side, :]
+        block = n[side, :]
+        gy = gy_all[side, :]
         pre = dot_nn(block, up_ref[stream])
         square = pre * pre
         bent = jnp.tanh(GELU_A * (pre + GELU_B * (square * pre)))
         half = 0.5 * (1.0 + bent)
         hidden = (pre * half).astype(BF16)
         slope = half + 0.5 * pre * (1.0 - bent * bent) * (GELU_A * (1.0 + 3.0 * GELU_B * square))
-        out_ref[0, side, :] = dot_nn(hidden, down_ref[stream]).astype(BF16)
+        out[side, :] = dot_nn(hidden, down_ref[stream]).astype(BF16)
         g_pre = (dot_nt(gy, down_ref[stream]) * slope).astype(BF16)
-        part_ref[0, side, :] = dot_nt(g_pre, up_ref[stream]).astype(BF16)
+        part[side, :] = dot_nt(g_pre, up_ref[stream]).astype(BF16)
         at = stream * depth
         acc[at : at + depth, :] += dot_tn(block, g_pre)
         at = 2 * depth + stream * hid
         acc[at : at + hid, :] += dot_tn(hidden, gy)
+    place(step, out_refs, out)
+    place(step, part_refs, part)
 
     @pl.when(step == pl.num_programs(0) - 1)
     def _():
@@ -201,102 +232,122 @@
     return pl.CostEstimate(flops=int(flops), bytes_accessed=int(size), transcendentals=0)
 
 
-def attend(rows_all, weights, out_weights, keep, tlen, vlen, pages):
-    blocks, rows, depth = rows_all.shape
+def attend(blocks, weights, out_weights, keep, tlen, vlen, pages):
+    rows, depth = blocks[0].shape
     width = out_weights.shape[1]
-    args = [rows_all, weights, out_weights]
-    specs = [per_block(rows_all.shape), whole(weights.shape), whole(out_weights.shape)]
+    args = [*blocks, weights, out_weights]
+    specs = [whole(a.shape) for a in args]
     if keep is not None:
         args.append(keep)
         specs.append(per_block(keep.shape))
-    outs = (
-        jax.ShapeDtypeStruct((blocks, rows, depth), BF16),
-        jax.ShapeDtypeStruct((blocks, 4, rows, width), BF16),
-    )
+    outs = [jax.ShapeDtypeStruct((rows, depth), BF16)] * 4
+    outs.append(jax.ShapeDtypeStruct((4, 4, rows, width), BF16))
 
     def body(*refs):
         attend_kernel(keep is not None, tlen, vlen, pages, *refs)
 
-    return pl.pallas_call(
+    *parts, saved = pl.pallas_call(
         body,
-        grid=(blocks,),
+        grid=(4,),
         in_specs=specs,
-        out_specs=tuple(per_block(o.shape) for o in outs),
+        out_specs=[whole(o.shape) for o in outs[:4]] + [per_block(outs[4].shape)],
         out_shape=outs,
-        cost_estimate=cost(2 * blocks * rows * (4 * depth * width + 1536 * width), args + list(outs)),
+        scratch_shapes=[pltpu.VMEM((rows, depth), BF16)] * 2,
+        cost_estimate=cost(8 * rows * (4 * depth * width + 1536 * width), args + outs),
         name="attend_cross" if keep is not None else "attend_self",
     )(*args)
-
-
-def attend_back(rows_all, grad_all, saved, weights, out_weights, keep, tlen, vlen, pages):
-    blocks, rows, depth = rows_all.shape
+    return parts, saved
+
+
+def attend_back(blocks, grad_blocks, saved, weights, out_weights, keep, tlen, vlen, pages):
+    rows, depth = blocks[0].shape
     width = out_weights.shape[1]
-    args = [rows_all, grad_all, saved, weights, out_weights]
-    specs = [per_block(a.shape) for a in args[:3]] + [whole(a.shape) for a in args[3:]]
+    args = [*blocks, *grad_blocks, saved, weights, out_weights]
+    specs = [whole(a.shape) for a in args]
+    specs[8] = per_block(saved.shape)
     if keep is not None:
         args.append(keep)
         specs.append(per_block(keep.shape))
-    outs = (
-        jax.ShapeDtypeStruct((blocks, rows, depth), BF16),
-        jax.ShapeDtypeStruct((8 * width, depth), BF16),
-    )
+    outs = [jax.ShapeDtypeStruct((rows, depth), BF16)] * 4
+    outs.append(jax.ShapeDtypeStruct((8 * width, depth), BF16))
 
     def body(*refs):
         attend_back_kernel(keep is not None, tlen, vlen, pages, *refs)
 
-    return pl.pallas_call(
+    *parts, grads = pl.pallas_call(
         body,
-        grid=(blocks,),
+        grid=(4,),
         in_specs=specs,
-        out_specs=(per_block(outs[0].shape), whole(outs[1].shape)),
+        out_specs=[whole(o.shape) for o in outs],
         out_shape=outs,
         scratch_shapes=[
+            pltpu.VMEM((rows, depth), BF16),
+            pltpu.VMEM((rows, depth), BF16),
             pltpu.VMEM((rows, width), BF16),
             pltpu.VMEM((3, rows, width), BF16),
             pltpu.VMEM((8 * width, depth), F32),
         ],
-        cost_estimate=cost(2 * blocks * rows * (8 * depth * width + 4096 * width), args + list(outs)),
+        cost_estimate=cost(8 * rows * (8 * depth * width + 4096 * width), args + outs),
         name="attend_cross_back" if keep is not None else "attend_self_back",
     )(*args)
-
-
-def feed(rows_all, grad_all, up, down, trows):
-    blocks, rows, depth = rows_all.shape
+    return parts, grads
+
+
+def feed(blocks, grad_blocks, up, down, trows):
+    rows, depth = blocks[0].shape
     hid = up.shape[2]
-    args = [rows_all, grad_all, up, down]
-    outs = (
-        jax.ShapeDtypeStruct((blocks, rows, depth), BF16),
-        jax.ShapeDtypeStruct((blocks, rows, depth), BF16),
-        jax.ShapeDtypeStruct((2 * depth + 2 * hid, depth), BF16),
-    )
+    args = [*blocks, *grad_blocks, up, down]
+    outs = [jax.ShapeDtypeStruct((rows, depth), BF16)] * 8
+    outs.append(jax.ShapeDtypeStruct((2 * depth + 2 * hid, depth), BF16))
 
     def body(*refs):
         feed_kernel(trows, *refs)
 
-    return pl.pallas_call(
+    results = pl.pallas_call(
         body,
-        grid=(blocks,),
-        in_specs=[per_block(a.shape) for a in args[:2]] + [whole(a.shape) for a in args[2:]],
-        out_specs=(per_block(outs[0].shape), per_block(outs[1].shape), whole(outs[2].shape)),
+        grid=(4,),
+        in_specs=[whole(a.shape) for a in args],
+        out_specs=[whole(o.shape) for o in outs],
         out_shape=outs,
-        scratch_shapes=[pltpu.VMEM((2 * depth + 2 * hid, depth), F32)],
-        cost_estimate=cost(2 * blocks * rows * 6 * depth * hid, args + list(outs)),
+        scratch_shapes=[pltpu.VMEM((rows, depth), BF16)] * 4
+        + [pltpu.VMEM((2 * depth + 2 * hid, depth), F32)],
+        cost_estimate=cost(8 * rows * 6 * depth * hid, args + outs),
         name="feed_both",
     )(*args)
+    return results[:4], results[4:8], results[8]
 
 
 def swap(values, axis, bit, size):
     return lax.ppermute(values, axis, [(i, i ^ bit) for i in range(size)])
 
 
-def gather_rows(values):
-    pair = jnp.stack([values, swap(values, "mp", 2, 4)])
-    return jnp.concatenate([pair, swap(pair, "mp", 1, 4)])
-
-
-def scatter_rows(parts):
-    pair = parts[:2].astype(F32) + swap(parts[2:], "mp", 1, 4).astype(F32)
-    return pair[0] + swap(pair[1].astype(BF16), "mp", 2, 4).astype(F32)
+def after(values, *earlier):
+    earlier = [e for e in earlier if e is not None]
+    if not earlier:
+        return values
+    return lax.optimization_barrier((values, earlier))[0]
+
+
+def gather_start(values):
+    return values, swap(values, "mp", 2, 4), swap(values, "mp", 1, 4)
+
+
+def gather_end(started, *earlier):
+    values, far, near = started
+    far = after(far, *earlier)
+    return [values, far, near, swap(far, "mp", 1, 4)]
+
+
+def scatter_start(parts):
+    own, far, near, both = parts
+    send = (far.astype(F32) + swap(both, "mp", 1, 4).astype(F32)).astype(BF16)
+    return own, swap(near, "mp", 1, 4), swap(send, "mp", 2, 4), send
+
+
+def scatter_end(started, *earlier):
+    own, near, far, _ = started
+    far = after(far, *earlier)
+    return own.astype(F32) + near.astype(F32) + far.astype(F32)
 
 
 def moments(values):
@@ -321,9 +372,42 @@
     return delta, grad * scaled
 
 
-def reduce_grads(grads, count):
-    total = lax.psum(grads, "dp")
-    return total.astype(F32)
+class Ring:
+    def __init__(self, grads, count):
+        self.shape, self.count = grads.shape, count
+        self.mine = lax.psum_scatter(grads, "dp", scatter_dimension=0, tiled=True)
+        self.right = self.left = self.mine
+        self.hops = 0
+        self.pieces = [(self.mine, 0)]
+        self.order = list(range(0, count, 2)) + list(range(count - 1, 0, -2))
+
+    def hop(self):
+        order, count = self.order, self.count
+        if self.hops >= count // 2:
+            return
+        self.hops += 1
+        onward = [(order[k], order[(k + 1) % count]) for k in range(count)]
+        self.right = lax.ppermute(self.right, "dp", onward)
+        self.pieces.append((self.right, count - self.hops))
+        if self.hops < count - count // 2:
+            self.left = lax.ppermute(self.left, "dp", [(b, a) for a, b in onward])
+            self.pieces.append((self.left, self.hops))
+
+    def state(self):
+        return (self.right, self.left)
+
+    def total(self):
+        while self.hops < self.count // 2:
+            self.hop()
+        at = lax.axis_index("dp")
+        position = jnp.array([self.order.index(i) for i in range(self.count)], jnp.int32)[at]
+        device_at = jnp.array(self.order, jnp.int32)
+        total = jnp.zeros(self.shape, F32)
+        length = self.mine.shape[0]
+        for piece, offset in self.pieces:
+            row = device_at[(position + offset) % self.count] * length
+            total = lax.dynamic_update_slice(total, piece.astype(F32), (row, 0))
+        return total
 
 
 def per_device(count, *arrays):
@@ -388,9 +472,21 @@
     inputs = [list(now), None, None]
     gathered = [[None] * CHUNKS for _ in range(3)]
     saved = [[None] * CHUNKS for _ in range(2)]
+    gates = [None] * CHUNKS
+    cots = [gather_start(cotangents[c]) for c in range(CHUNKS)]
     for s in range(2):
+        started = []
         for c in range(CHUNKS):
-            gathered[s][c] = gather_rows(normalize(now[c], gains[s], shifts[s]))
+            if s:
+                now[c] = now[c] + scatter_end(ended[c], gates[-1])
+                inputs[s][c] = now[c]
+            started.append(gather_start(normalize(now[c], gains[s], shifts[s])))
+        inputs[s + 1] = [None] * CHUNKS
+        ended = []
+        previous = None
+        for c in range(CHUNKS):
+            gate = cots[s][1] if c == CHUNKS - 1 else None
+            gathered[s][c] = gather_end(started[c], previous, gate)
             parts, saved[s][c] = attend(
                 gathered[s][c],
                 weights[s],
@@ -400,15 +496,15 @@
                 vlen,
                 pages,
             )
-            now[c] = now[c] + scatter_rows(parts)
-        inputs[s + 1] = list(now)
+            gates[c] = parts[0]
+            ended.append(scatter_start(parts))
+            previous = ended[c][3]
     grads_now = [v.astype(F32) for v in cotangents]
-    totals = [None] * 3
     scale_sums = [None] * 3
     shift_sums = [None] * 3
 
-    def back(s, c, parts):
-        grad = scatter_rows(parts)
+    def back(s, c, ended, *earlier):
+        grad = scatter_end(ended, gates[-1], *earlier)
         delta, product = normalize_back(inputs[s][c], gains[s], grad)
         grads_now[c] = grads_now[c] + delta
         sums = [jnp.sum(v, axis=0) for v in (product[:trows], product[trows:])]
@@ -417,22 +513,38 @@
         scale_sums[s] = sums if scale_sums[s] is None else scale_sums[s] + sums
         shift_sums[s] = shifts if shift_sums[s] is None else shift_sums[s] + shifts
 
-    partial = []
+    started = []
     for c in range(CHUNKS):
-        cot = gather_rows(cotangents[c])
-        rows_all = gather_rows(normalize(now[c], gains[2], shifts[2]))
+        now[c] = now[c] + scatter_end(ended[c], gates[-1])
+        inputs[2][c] = now[c]
+        started.append(gather_start(normalize(now[c], gains[2], shifts[2])))
+    partial, ended, outputs = [], [], []
+    previous = None
+    for c in range(CHUNKS):
+        rows_all = gather_end(started[c], previous)
+        cot = gather_end(cots[c])
         out, parts, grads = feed(rows_all, cot, up_weight, down_weight, trows)
+        gates[c] = parts[0]
         partial.append(grads.astype(F32))
-        back(2, c, parts)
-        now[c] = now[c] + scatter_rows(out)
-    totals[2] = reduce_grads(sum(partial).astype(BF16), count)
+        ended.append(scatter_start(parts))
+        previous = ended[c][3]
+        outputs.append(out)
+    rings = [None, None, Ring(sum(partial).astype(BF16), count)]
     for s in (1, 0):
-        partial = []
+        started = []
         for c in range(CHUNKS):
-            grad_all = gather_rows(grads_now[c].astype(BF16))
+            back(s + 1, c, ended[c])
+            started.append(gather_start(grads_now[c].astype(BF16)))
+        partial, ended = [], []
+        previous = None
+        for c in range(CHUNKS):
+            gate = None
+            if s == 0:
+                gate = rings[2].state()
+                rings[2].hop()
             parts, grads = attend_back(
                 gathered[s][c],
-                grad_all,
+                gather_end(started[c], previous, gate),
                 saved[s][c],
                 weights[s],
                 outs[s],
@@ -441,9 +553,19 @@
                 vlen,
                 pages,
             )
+            if c == 0:
+                outputs[1 - s] = scatter_start(after(outputs[1 - s], parts[0]))
+            gates[c] = parts[0]
             partial.append(grads.astype(F32))
-            back(s, c, parts)
-        totals[s] = reduce_grads(sum(partial).astype(BF16), count)
+            ended.append(scatter_start(parts))
+            previous = ended[c][3]
+        rings[s] = Ring(after(sum(partial).astype(BF16), rings[s + 1].mine), count)
+    for c in range(CHUNKS):
+        gate = rings[2].state()
+        rings[2].hop()
+        back(0, c, ended[c], gate)
+        now[c] = now[c] + scatter_end(outputs[c])
+    totals = [ring.total() for ring in rings]
 
     small = jnp.concatenate(scale_sums + shift_sums)
     for bit in (1, 2):

time: 979 us -> 785 us (0.80)
  waiting for transfers between devices: 555 us -> 304 us
  starting transfers between devices: 43.4 us -> 66.4 us
  Pallas kernels: 202 us -> 225 us
  between operations: 16.3 us -> 32.5 us
    psum x1 -> x0, waiting for transfers between devices: 233 us -> none  [reduce_grads(): total = lax.psum(grads, 'dp')]
    ppermute x53 -> x77, waiting for transfers between devices: 322 us -> 223 us  [swap(): return lax.ppermute(values, axis, [(i, i ^ bit) for i in range(size)])]
    ppermute x0 -> x21, waiting for transfers between devices: none -> 65.5 us  [the longest x12 35.6 us: hop(): self.right = lax.ppermute(self.right, 'dp', onward)]
    concatenate x12 -> x2, other arithmetic: 29 us -> 0.08 us  [join(): return [jnp.concatenate([text[c], visual[c]]) for c in range(CHUNKS)]]
    ppermute x0 -> x21, starting transfers between devices: none -> 24.3 us  [the longest x9 15.2 us: hop(): self.left = lax.ppermute(self.left, 'dp', [(b, a) for a, b in onward])]
    pallas_call x10, Pallas kernels: 202 us -> 225 us  [the longest x4 115 us: attend_back(): pl.pallas_call(body, grid=(4,), in_specs=specs, out_specs=[whole(o.shape)...]
    dynamic_update_slice x0 -> x24, other arithmetic: none -> 20.6 us  [total(): total = lax.dynamic_update_slice(total, piece.astype(F32), (row, 0))]
    slice x12 -> x0, local copies, waits for them, and re-layouts: 17.7 us -> none  [scatter_rows(): pair = parts[:2].astype(F32) + swap(parts[2:], 'mp', 1, 4).astype(F32)]
  transfers between devices with their start and end apart: 54 -> 101, of which waited for: 25 -> 42; matrix products, arithmetic and copies ran while one was open for 11% -> 15% of each run, Pallas kernels for 18% -> 20%
where the time goes in v3:
time: 785 us; the launch traced here: 781 us
  waiting for transfers between devices  304 us (39%)
  Pallas kernels  225 us (29%)
  other arithmetic  96.5 us (12%)
  starting transfers between devices  66.4 us (8%)
  local copies, waits for them, and re-layouts  56.7 us (7%)
  between operations  32.5 us (4%)
    ppermute x77, waiting for transfers between devices, swap(): return lax.ppermute(values, axis, [(i, i ^ bit) for i in range(size)])  223 us
    pallas_call x4, Pallas kernels, attend_back(): pl.pallas_call(body, grid=(4,), in_specs=specs, out_specs=[whole(o.shape)...  115 us
    pallas_call x4, Pallas kernels, attend(): pl.pallas_call(body, grid=(4,), in_specs=specs, out_specs=[whole(o.shape)...  57.2 us
    pallas_call x2, Pallas kernels, feed(): pl.pallas_call(body, grid=(4,), in_specs=[whole(a.shape) for a in args],...  52.8 us
    ppermute x77, starting transfers between devices, swap(): return lax.ppermute(values, axis, [(i, i ^ bit) for i in range(size)])  41.9 us
    ppermute x12, waiting for transfers between devices, hop(): self.right = lax.ppermute(self.right, 'dp', onward)  35.6 us
    ppermute x9, waiting for transfers between devices, hop(): self.left = lax.ppermute(self.left, 'dp', [(b, a) for a, b in onward])  30 us
    unnamed x211, local copies, waits for them, and re-layouts  21.5 us
  transfers between devices with their start and end apart: 101, of which 42 were waited for; matrix products, arithmetic and copies ran while one was open for 15% of the time, Pallas kernels for 20%

profile of v3, /device:TPU:0, one launch (start us, length us, event | category | flops | bytes accessed | tf_op | source)
XLA Modules:
  0.0 781.0 jit_solution(3996288387601759921)
XLA Ops:
  35.2 13.8 %attend_cross.2 = (bf16[416,768]{1,0:T(8,128)(2,1)}, bf16[416,768]{1,0:T(8,128)(2,1)}, bf16[416,768]{1,0:T(8,128)(2,1)}, bf16[416,768]{1,0:T(8,128)(2,1)}, bf16[4,4,416,192]{3,2,1,0:T(8,128)(2,1)}) custom-call(bf16[416,768]{1,0:T(8,128)(2,1)} %get-tuple-element.266.refs_0_, bf16[416,768]{1,0:T(8,128)(2,1)} %collective-permute-done.refs_1_, ...), custom_call_target="tpu_custom_call" | custom-call | flops 2944401408 | bytes 10033664 | tf_op jit(solution)/shard_map/attend_cross/pallas_call | solution.py:249
  52.6 14.4 %collective-permute-done.7.refs_5_ = bf16[416,768]{1,0:T(8,128)(2,1)S(1)} collective-permute-done((bf16[416,768]{1,0:T(8,128)(2,1)S(1)}, bf16[416,768]{1,0:T(8,128)(2,1)S(1)}, u32[]{:S(2)}, u32[]{:S(2)}) %collective-permute-start.7) | collective-permute-done | bytes 639008 | tf_op jit(solution)/shard_map/ppermute | solution.py:321
  72.0 13.7 %attend_cross.3 = (bf16[416,768]{1,0:T(8,128)(2,1)}, bf16[416,768]{1,0:T(8,128)(2,1)}, bf16[416,768]{1,0:T(8,128)(2,1)}, bf16[416,768]{1,0:T(8,128)(2,1)}, bf16[4,4,416,192]{3,2,1,0:T(8,128)(2,1)}) custom-call(bf16[416,768]{1,0:T(8,128)(2,1)} %get-tuple-element.267.refs_0_, bf16[416,768]{1,0:T(8,128)(2,1)} %collective-permute-done.6.refs_1_, ...), custom_call_target="tpu_custom_call" | custom-call | flops 2944401408 | bytes 10033664 | tf_op jit(solution)/shard_map/attend_cross/pallas_call | solution.py:249
  91.6 14.1 %collective-permute-done.18 = bf16[416,768]{1,0:T(8,128)(2,1)S(1)} collective-permute-done((bf16[416,768]{1,0:T(8,128)(2,1)S(1)}, bf16[416,768]{1,0:T(8,128)(2,1)S(1)}, u32[]{:S(2)}, u32[]{:S(2)}) %collective-permute-start.18) | collective-permute-done | bytes 639008 | tf_op jit(solution)/shard_map/ppermute | solution.py:321
  108.2 15.3 %collective-permute-done.10.refs_1_ = bf16[416,768]{1,0:T(8,128)(2,1)S(1)} collective-permute-done((bf16[416,768]{1,0:T(8,128)(2,1)S(1)}, bf16[416,768]{1,0:T(8,128)(2,1)S(1)}, u32[]{:S(2)}, u32[]{:S(2)}) %collective-permute-start.10) | collective-permute-done | bytes 639008 | tf_op jit(solution)/shard_map/ppermute | solution.py:321
  126.8 14.9 %attend_self.2 = (bf16[416,768]{1,0:T(8,128)(2,1)}, bf16[416,768]{1,0:T(8,128)(2,1)}, bf16[416,768]{1,0:T(8,128)(2,1)}, bf16[416,768]{1,0:T(8,128)(2,1)}, bf16[4,4,416,192]{3,2,1,0:T(8,128)(2,1)}) custom-call(bf16[416,768]{1,0:T(8,128)(2,1)} %copy-done.43, bf16[416,768]{1,0:T(8,128)(2,1)} %copy-done.82, bf16[416,768]{1,0:T(8,128)(2,1)} %copy-done.83, ...), custom_call_target="tpu_custom_call" | custom-call | flops 2944401408 | bytes 10027008 | tf_op jit(solution)/shard_map/attend_self/pallas_call | solution.py:249
  144.7 15.1 %collective-permute-done.20.refs_5_ = bf16[416,768]{1,0:T(8,128)(2,1)S(1)} collective-permute-done((bf16[416,768]{1,0:T(8,128)(2,1)S(1)}, bf16[416,768]{1,0:T(8,128)(2,1)S(1)}, u32[]{:S(2)}, u32[]{:S(2)}) %collective-permute-start.20) | collective-permute-done | bytes 639008 | tf_op jit(solution)/shard_map/ppermute | solution.py:321
  159.7 12.8 %collective-permute-done.19.refs_1_ = bf16[416,768]{1,0:T(8,128)(2,1)S(1)} collective-permute-done((bf16[416,768]{1,0:T(8,128)(2,1)S(1)}, bf16[416,768]{1,0:T(8,128)(2,1)S(1)}, u32[]{:S(2)}, u32[]{:S(2)}) %collective-permute-start.19) | collective-permute-done | bytes 639008 | tf_op jit(solution)/shard_map/ppermute | solution.py:321
  174.7 14.7 %attend_self.3 = (bf16[416,768]{1,0:T(8,128)(2,1)}, bf16[416,768]{1,0:T(8,128)(2,1)}, bf16[416,768]{1,0:T(8,128)(2,1)}, bf16[416,768]{1,0:T(8,128)(2,1)}, bf16[4,4,416,192]{3,2,1,0:T(8,128)(2,1)}) custom-call(bf16[416,768]{1,0:T(8,128)(2,1)} %get-tuple-element.265.refs_0_, bf16[416,768]{1,0:T(8,128)(2,1)} %copy-done.80, bf16[416,768]{1,0:T(8,128)(2,1)} %copy-done.81, ...), custom_call_target="tpu_custom_call" | custom-call | flops 2944401408 | bytes 10027008 | tf_op jit(solution)/shard_map/attend_self/pallas_call | solution.py:249
  195.6 13.8 %collective-permute-done.33 = bf16[416,768]{1,0:T(8,128)(2,1)S(1)} collective-permute-done((bf16[416,768]{1,0:T(8,128)(2,1)S(1)}, bf16[416,768]{1,0:T(8,128)(2,1)S(1)}, u32[]{:S(2)}, u32[]{:S(2)}) %collective-permute-start.33) | collective-permute-done | bytes 639008 | tf_op jit(solution)/shard_map/ppermute | solution.py:321
  213.0 14.2 %collective-permute-done.23.refs_1_ = bf16[416,768]{1,0:T(8,128)(2,1)S(1)} collective-permute-done((bf16[416,768]{1,0:T(8,128)(2,1)S(1)}, bf16[416,768]{1,0:T(8,128)(2,1)S(1)}, u32[]{:S(2)}, u32[]{:S(2)}) %collective-permute-start.23) | collective-permute-done | bytes 639008 | tf_op jit(solution)/shard_map/ppermute | solution.py:321
  229.4 26.2 %feed_both.2 = (bf16[416,768]{1,0:T(8,128)(2,1)}, bf16[416,768]{1,0:T(8,128)(2,1)}, bf16[416,768]{1,0:T(8,128)(2,1)}, bf16[416,768]{1,0:T(8,128)(2,1)}, bf16[416...) custom-call(bf16[416,768]{1,0:T(8,128)(2,1)} %copy-done.48, ...), custom_call_target="tpu_custom_call" | custom-call | flops 11777605632 | bytes 19660800 | tf_op jit(solution)/shard_map/feed_both/pallas_call | solution.py:306
  260.0 12.7 %collective-permute-done.34.refs_1_ = bf16[416,768]{1,0:T(8,128)(2,1)S(1)} collective-permute-done((bf16[416,768]{1,0:T(8,128)(2,1)}, bf16[416,768]{1,0:T(8,128)(2,1)S(1)}, u32[]{:S(2)}, u32[]{:S(2)}) %collective-permute-start.34) | collective-permute-done | bytes 639008 | tf_op jit(solution)/shard_map/ppermute | solution.py:321
  275.7 26.6 %feed_both.3 = (bf16[416,768]{1,0:T(8,128)(2,1)}, bf16[416,768]{1,0:T(8,128)(2,1)}, bf16[416,768]{1,0:T(8,128)(2,1)}, bf16[416,768]{1,0:T(8,128)(2,1)}, bf16[416...) custom-call(bf16[416,768]{1,0:T(8,128)(2,1)} %get-tuple-element.263., ...), custom_call_target="tpu_custom_call" | custom-call | flops 11777605632 | bytes 19660800 | tf_op jit(solution)/shard_map/feed_both/pallas_call | solution.py:306
  306.9 13.1 %collective-permute-done.30 = bf16[416,768]{1,0:T(8,128)(2,1)S(1)} collective-permute-done((bf16[416,768]{1,0:T(8,128)(2,1)}, bf16[416,768]{1,0:T(8,128)(2,1)S(1)}, u32[]{:S(2)}, u32[]{:S(2)}) %collective-permute-start.30) | collective-permute-done | bytes 639008 | tf_op jit(solution)/shard_map/ppermute | solution.py:321
  374.8 28.5 %attend_self_back.2 = (bf16[416,768]{1,0:T(8,128)(2,1)}, bf16[416,768]{1,0:T(8,128)(2,1)}, bf16[416,768]{1,0:T(8,128)(2,1)}, bf16[416,768]{1,0:T(8,128)(2,1)}, bf16[1536,768]{1,0:T(8,128)(2,1)}) custom-call(bf16[416,768]{1,0:T(8,128)(2,1)} %copy-done.43, bf16[416,768]{1,0:T(8,128)(2,1)} %copy-done.82, bf16[416,768]{1,0:T(8,128)(2,1)} %copy-done.83, ...), custom_call_target="tpu_custom_call" | custom-call | flops 6543114240 | bytes 14942208 | tf_op jit(solution)/shard_map/attend_self_back/pallas_call | solution.py:277
  410.4 12.7 %collective-permute-done.51.refs_5_ = bf16[416,768]{1,0:T(8,128)(2,1)S(1)} collective-permute-done((bf16[416,768]{1,0:T(8,128)(2,1)}, bf16[416,768]{1,0:T(8,128)(2,1)S(1)}, u32[]{:S(2)}, u32[]{:S(2)}) %collective-permute-start.51) | collective-permute-done | bytes 639008 | tf_op jit(solution)/shard_map/ppermute | solution.py:321
  427.9 28.5 %attend_self_back.3 = (bf16[416,768]{1,0:T(8,128)(2,1)}, bf16[416,768]{1,0:T(8,128)(2,1)}, bf16[416,768]{1,0:T(8,128)(2,1)}, bf16[416,768]{1,0:T(8,128)(2,1)}, bf16[1536,768]{1,0:T(8,128)(2,1)}) custom-call(bf16[416,768]{1,0:T(8,128)(2,1)} %get-tuple-element.265.refs_0_, bf16[416,768]{1,0:T(8,128)(2,1)} %copy-done.80, bf16[416,768]{1,0:T(8,128)(2,1)} %copy-done.81, ...), custom_call_target="tpu_custom_call" | custom-call | flops 6543114240 | bytes 14942208 | tf_op jit(solution)/shard_map/attend_self_back/pallas_call | solution.py:277
  467.5 13.6 %collective-permute-done.65 = bf16[416,768]{1,0:T(8,128)(2,1)} collective-permute-done((bf16[416,768]{1,0:T(8,128)(2,1)}, bf16[416,768]{1,0:T(8,128)(2,1)}, u32[]{:S(2)}, u32[]{:S(2)}) %collective-permute-start.65) | collective-permute-done | bytes 639008 | tf_op jit(solution)/shard_map/ppermute | solution.py:321
  514.3 14.1 %collective-permute-done.68 = bf16[384,768]{1,0:T(8,128)(2,1)} collective-permute-done((bf16[384,768]{1,0:T(8,128)(2,1)}, bf16[384,768]{1,0:T(8,128)(2,1)}, u32[]{:S(2)}, u32[]{:S(2)}) %collective-permute-start.68) | collective-permute-done | bytes 589856 | tf_op jit(solution)/shard_map/ppermute | solution.py:393
  528.7 29.1 %attend_cross_back.2 = (bf16[416,768]{1,0:T(8,128)(2,1)}, bf16[416,768]{1,0:T(8,128)(2,1)}, bf16[416,768]{1,0:T(8,128)(2,1)}, bf16[416,768]{1,0:T(8,128)(2,1)}, bf16[1536,768]{1,0:T(8,128)(2,1)}) custom-call(bf16[416,768]{1,0:T(8,128)(2,1)} %get-tuple-element.266.refs_0_, bf16[416,768]{1,0:T(8,128)(2,1)} %collective-permute-done.refs_1_, ...), custom_call_target="tpu_custom_call" | custom-call | flops 6543114240 | bytes 14948864 | tf_op jit(solution)/shard_map/attend_cross_back/pallas_call | solution.py:277
  570.3 13.7 %collective-permute-done.76 = bf16[384,768]{1,0:T(8,128)(2,1)} collective-permute-done((bf16[384,768]{1,0:T(8,128)(2,1)}, bf16[384,768]{1,0:T(8,128)(2,1)}, u32[]{:S(2)}, u32[]{:S(2)}) %collective-permute-start.76) | collective-permute-done | bytes 589856 | tf_op jit(solution)/shard_map/ppermute | solution.py:390
  593.0 29.0 %attend_cross_back.3 = (bf16[416,768]{1,0:T(8,128)(2,1)}, bf16[416,768]{1,0:T(8,128)(2,1)}, bf16[416,768]{1,0:T(8,128)(2,1)}, bf16[416,768]{1,0:T(8,128)(2,1)}, bf16[1536,768]{1,0:T(8,128)(2,1)}) custom-call(bf16[416,768]{1,0:T(8,128)(2,1)} %get-tuple-element.267.refs_0_, bf16[416,768]{1,0:T(8,128)(2,1)} %collective-permute-done.6.refs_1_, ...), custom_call_target="tpu_custom_call" | custom-call | flops 6543114240 | bytes 14948864 | tf_op jit(solution)/shard_map/attend_cross_back/pallas_call | solution.py:277
  722.9 15.6 %reduce-scatter.8.cloned.1.call-done = bf16[192,768]{1,0:T(8,128)(2,1)} async-done(((bf16[1536,768]{1,0:T(8,128)(2,1)}), bf16[192,768]{1,0:T(8,128)(2,1)}) %reduce-scatter.8.cloned.1.call-update) | async-done | bytes 294928 | tf_op jit(solution)/shard_map/reduce_scatter | solution.py:378
  (615 shorter events, 328.4 us)
Async XLA Ops:
  7.2 483.0 %reduce-scatter.4.cloned.1.call-start = ((), (), s32[]{:S(2)}) async-start(), calls=%async_computation.3 | async-start | bytes 5308416 | tf_op jit(solution)/shard_map/reduce_scatter | solution.py:378
  14.4 38.2 %collective-permute-start.6 = (bf16[416,768]{1,0:T(8,128)(2,1)}, bf16[416,768]{1,0:T(8,128)(2,1)}, u32[]{:S(2)}, u32[]{:S(2)}) collective-permute-start(bf16[416,768]{1,0:T(8,128)(2,1)} %get-tuple-element.267.refs_0_), channel_id=1, source_target_pairs={{0,2},{1,3},{2,0},{3,1},{4,6},{5,7},{6,4},{7,5},{8,10},{9,11},{10,... | collective-permute-start | bytes 1916936 | tf_op jit(solution)/shard_map/ppermute | solution.py:321
  142.9 29.6 %collective-permute-start.19 = (bf16[416,768]{1,0:T(8,128)(2,1)S(1)}, bf16[416,768]{1,0:T(8,128)(2,1)S(1)}, u32[]{:S(2)}, u32[]{:S(2)}) collective-permute-start(bf16[416,768]{1,0:T(8,128)(2,1)S(1)} %copy-done.42), channel_id=1, source_target_pairs={{0,2},{1,3},{2,0},{3,1},{4,6},{5,7},{6,4},{7,5},{8,10},{9,11},{10,... | collective-permute-start | bytes 1916936 | tf_op jit(solution)/shard_map/ppermute | solution.py:321
  144.5 28.3 %collective-permute-start.21 = (bf16[416,768]{1,0:T(8,128)(2,1)S(1)}, bf16[416,768]{1,0:T(8,128)(2,1)S(1)}, u32[]{:S(2)}, u32[]{:S(2)}) collective-permute-start(bf16[416,768]{1,0:T(8,128)(2,1)S(1)} %copy-done.42), channel_id=1, source_target_pairs={{0,1},{1,0},{2,3},{3,2},{4,5},{5,4},{6,7},{7,6},{8,9},{9,8},{10,11... | collective-permute-start | bytes 1916936 | tf_op jit(solution)/shard_map/ppermute | solution.py:321
  305.9 27.2 %collective-permute-start.50 = (bf16[416,768]{1,0:T(8,128)(2,1)S(1)}, bf16[416,768]{1,0:T(8,128)(2,1)S(1)}, u32[]{:S(2)}, u32[]{:S(2)}) collective-permute-start(bf16[416,768]{1,0:T(8,128)(2,1)S(1)} %add_convert_fusion.8), channel_id=1, source_target_pairs={{0,2},{1,3},{2,0},{3,1},{4,6},{5,7},{6,4},{7,5},{8,10},{9,11},{10,... | collective-permute-start | bytes 1916936 | tf_op jit(solution)/shard_map/ppermute | solution.py:321
  306.9 26.2 %collective-permute-start.48 = (bf16[416,768]{1,0:T(8,128)(2,1)}, bf16[416,768]{1,0:T(8,128)(2,1)S(1)}, u32[]{:S(2)}, u32[]{:S(2)}) collective-permute-start(bf16[416,768]{1,0:T(8,128)(2,1)} %get-tuple-element.140), channel_id=1, source_target_pairs={{0,1},{1,0},{2,3},{3,2},{4,5},{5,4},{6,7},{7,6},{8,9},{9,8},{10,11... | collective-permute-start | bytes 1916936 | tf_op jit(solution)/shard_map/ppermute | solution.py:321
  344.0 313.7 %reduce-scatter.6.cloned.1.call-start = ((), (), s32[]{:S(2)}) async-start(), calls=%async_computation.4 | async-start | bytes 2654208 | tf_op jit(solution)/shard_map/reduce_scatter | solution.py:378
  344.0 30.8 %collective-permute-start.40 = (bf16[416,768]{1,0:T(8,128)(2,1)}, bf16[416,768]{1,0:T(8,128)(2,1)}, u32[]{:S(2)}, u32[]{:S(2)}) collective-permute-start(bf16[416,768]{1,0:T(8,128)(2,1)} %get-tuple-element.272.refs_4_), channel_id=1, source_target_pairs={{0,1},{1,0},{2,3},{3,2},{4,5},{5,4},{6,7},{7,6},{8,9},{9,8},{10,11... | collective-permute-start | bytes 1916936 | tf_op jit(solution)/shard_map/ppermute | solution.py:321
  423.2 33.2 %collective-permute-start.45 = (bf16[416,768]{1,0:T(8,128)(2,1)}, bf16[416,768]{1,0:T(8,128)(2,1)}, u32[]{:S(2)}, u32[]{:S(2)}) collective-permute-start(bf16[416,768]{1,0:T(8,128)(2,1)} %get-tuple-element.137), channel_id=1, source_target_pairs={{0,1},{1,0},{2,3},{3,2},{4,5},{5,4},{6,7},{7,6},{8,9},{9,8},{10,11... | collective-permute-start | bytes 1916936 | tf_op jit(solution)/shard_map/ppermute | solution.py:321
  423.8 35.3 %collective-permute-start.42 = (bf16[416,768]{1,0:T(8,128)(2,1)}, bf16[416,768]{1,0:T(8,128)(2,1)}, u32[]{:S(2)}, u32[]{:S(2)}) collective-permute-start(bf16[416,768]{1,0:T(8,128)(2,1)} %get-tuple-element.130), channel_id=1, source_target_pairs={{0,1},{1,0},{2,3},{3,2},{4,5},{5,4},{6,7},{7,6},{8,9},{9,8},{10,11... | collective-permute-start | bytes 1916936 | tf_op jit(solution)/shard_map/ppermute | solution.py:321
  423.9 32.5 %collective-permute-start.47 = (bf16[416,768]{1,0:T(8,128)(2,1)}, bf16[416,768]{1,0:T(8,128)(2,1)}, u32[]{:S(2)}, u32[]{:S(2)}) collective-permute-start(bf16[416,768]{1,0:T(8,128)(2,1)} %add_convert_fusion.9), channel_id=1, source_target_pairs={{0,2},{1,3},{2,0},{3,1},{4,6},{5,7},{6,4},{7,5},{8,10},{9,11},{10,... | collective-permute-start | bytes 1916936 | tf_op jit(solution)/shard_map/ppermute | solution.py:321
  425.9 33.3 %collective-permute-start.44 = (bf16[416,768]{1,0:T(8,128)(2,1)}, bf16[416,768]{1,0:T(8,128)(2,1)}, u32[]{:S(2)}, u32[]{:S(2)}) collective-permute-start(bf16[416,768]{1,0:T(8,128)(2,1)} %add_convert_fusion.11), channel_id=1, source_target_pairs={{0,2},{1,3},{2,0},{3,1},{4,6},{5,7},{6,4},{7,5},{8,10},{9,11},{10,... | collective-permute-start | bytes 1916936 | tf_op jit(solution)/shard_map/ppermute | solution.py:321
  489.0 24.8 %collective-permute-start.55 = (bf16[416,768]{1,0:T(8,128)(2,1)}, bf16[416,768]{1,0:T(8,128)(2,1)}, u32[]{:S(2)}, u32[]{:S(2)}) collective-permute-start(bf16[416,768]{1,0:T(8,128)(2,1)} %get-tuple-element.270.refs_4_), channel_id=1, source_target_pairs={{0,1},{1,0},{2,3},{3,2},{4,5},{5,4},{6,7},{7,6},{8,9},{9,8},{10,11... | collective-permute-start | bytes 1916936 | tf_op jit(solution)/shard_map/ppermute | solution.py:321
  489.1 79.6 %collective-permute-start.66 = (bf16[416,768]{1,0:T(8,128)(2,1)}, bf16[416,768]{1,0:T(8,128)(2,1)}, u32[]{:S(2)}, u32[]{:S(2)}) collective-permute-start(bf16[416,768]{1,0:T(8,128)(2,1)} %get-tuple-element.220.refs_4_), channel_id=1, source_target_pairs={{0,2},{1,3},{2,0},{3,1},{4,6},{5,7},{6,4},{7,5},{8,10},{9,11},{10,... | collective-permute-start | bytes 1916936 | tf_op jit(solution)/shard_map/ppermute | solution.py:321
  507.0 231.5 %reduce-scatter.8.cloned.1.call-start = ((), (), s32[]{:S(2)}) async-start(), calls=%async_computation.5 | async-start | bytes 2654208 | tf_op jit(solution)/shard_map/reduce_scatter | solution.py:378
  512.4 78.1 %collective-permute-start.69 = (bf16[416,768]{1,0:T(8,128)(2,1)}, bf16[416,768]{1,0:T(8,128)(2,1)}, u32[]{:S(2)}, u32[]{:S(2)}) collective-permute-start(bf16[416,768]{1,0:T(8,128)(2,1)} %get-tuple-element.220.refs_4_), channel_id=1, source_target_pairs={{0,1},{1,0},{2,3},{3,2},{4,5},{5,4},{6,7},{7,6},{8,9},{9,8},{10,11... | collective-permute-start | bytes 1916936 | tf_op jit(solution)/shard_map/ppermute | solution.py:321
  513.8 46.4 %collective-permute-start.71 = (bf16[384,768]{1,0:T(8,128)(2,1)S(1)}, bf16[384,768]{1,0:T(8,128)(2,1)}, u32[]{:S(2)}, u32[]{:S(2)}) collective-permute-start(bf16[384,768]{1,0:T(8,128)(2,1)S(1)} %collective-permute-done.67), channel_id=1, source_target_pairs={{0,8},{8,16},{16,24},{24,28},{28,20},{20,12},{12,4},{4,0},{1,9},{9... | collective-permute-start | bytes 1769480 | tf_op jit(solution)/shard_map/ppermute | solution.py:390
  528.4 34.3 %collective-permute-start.72 = (bf16[384,768]{1,0:T(8,128)(2,1)}, bf16[384,768]{1,0:T(8,128)(2,1)S(1)}, u32[]{:S(2)}, u32[]{:S(2)}) collective-permute-start(bf16[384,768]{1,0:T(8,128)(2,1)} %collective-permute-done.68), channel_id=1, source_target_pairs={{8,0},{16,8},{24,16},{28,24},{20,28},{12,20},{4,12},{0,4},{9,1},{1... | collective-permute-start | bytes 1769480 | tf_op jit(solution)/shard_map/ppermute | solution.py:393
  568.7 53.3 %collective-permute-start.60 = (bf16[416,768]{1,0:T(8,128)(2,1)}, bf16[416,768]{1,0:T(8,128)(2,1)}, u32[]{:S(2)}, u32[]{:S(2)}) collective-permute-start(bf16[416,768]{1,0:T(8,128)(2,1)} %get-tuple-element.157), channel_id=1, source_target_pairs={{0,1},{1,0},{2,3},{3,2},{4,5},{5,4},{6,7},{7,6},{8,9},{9,8},{10,11... | collective-permute-start | bytes 1916936 | tf_op jit(solution)/shard_map/ppermute | solution.py:321
  584.1 40.9 %collective-permute-start.57 = (bf16[416,768]{1,0:T(8,128)(2,1)}, bf16[416,768]{1,0:T(8,128)(2,1)}, u32[]{:S(2)}, u32[]{:S(2)}) collective-permute-start(bf16[416,768]{1,0:T(8,128)(2,1)} %get-tuple-element.154), channel_id=1, source_target_pairs={{0,1},{1,0},{2,3},{3,2},{4,5},{5,4},{6,7},{7,6},{8,9},{9,8},{10,11... | collective-permute-start | bytes 1916936 | tf_op jit(solution)/shard_map/ppermute | solution.py:321
  589.4 32.5 %collective-permute-start.62 = (bf16[416,768]{1,0:T(8,128)(2,1)S(1)}, bf16[416,768]{1,0:T(8,128)(2,1)S(1)}, u32[]{:S(2)}, u32[]{:S(2)}) collective-permute-start(bf16[416,768]{1,0:T(8,128)(2,1)S(1)} %add_convert_fusion.5), channel_id=1, source_target_pairs={{0,2},{1,3},{2,0},{3,1},{4,6},{5,7},{6,4},{7,5},{8,10},{9,11},{10,... | collective-permute-start | bytes 1916936 | tf_op jit(solution)/shard_map/ppermute | solution.py:321
  590.5 34.4 %collective-permute-start.59 = (bf16[416,768]{1,0:T(8,128)(2,1)}, bf16[416,768]{1,0:T(8,128)(2,1)}, u32[]{:S(2)}, u32[]{:S(2)}) collective-permute-start(bf16[416,768]{1,0:T(8,128)(2,1)} %add_convert_fusion.7), channel_id=1, source_target_pairs={{0,2},{1,3},{2,0},{3,1},{4,6},{5,7},{6,4},{7,5},{8,10},{9,11},{10,... | collective-permute-start | bytes 1916936 | tf_op jit(solution)/shard_map/ppermute | solution.py:321
  592.6 42.7 %collective-permute-start.92 = (bf16[384,768]{1,0:T(8,128)(2,1)}, bf16[384,768]{1,0:T(8,128)(2,1)}, u32[]{:S(2)}, u32[]{:S(2)}) collective-permute-start(bf16[384,768]{1,0:T(8,128)(2,1)} %collective-permute-done.76), channel_id=1, source_target_pairs={{0,8},{8,16},{16,24},{24,28},{28,20},{20,12},{12,4},{4,0},{1,9},{9... | collective-permute-start | bytes 1769480 | tf_op jit(solution)/shard_map/ppermute | solution.py:390
  622.7 32.9 %collective-permute-start.73 = (bf16[416,768]{1,0:T(8,128)(2,1)}, bf16[416,768]{1,0:T(8,128)(2,1)}, u32[]{:S(2)}, u32[]{:S(2)}) collective-permute-start(bf16[416,768]{1,0:T(8,128)(2,1)} %get-tuple-element.168), channel_id=1, source_target_pairs={{0,1},{1,0},{2,3},{3,2},{4,5},{5,4},{6,7},{7,6},{8,9},{9,8},{10,11... | collective-permute-start | bytes 1916936 | tf_op jit(solution)/shard_map/ppermute | solution.py:321
  (182 other events, 1682.6 us)
Sparse Core Ops, SparseCore 0:
  344.1 96.5 reduce-scatter.3
  507.1 85.4 reduce-scatter.5
  657.8 80.6 reduce-scatter.7
